TPU v7x, 32 devices: a whole 2x2x4 slice. The times are simulated.
32 devices in a mesh: brick: 16 (over z, y, core), view: 2 (over x).
Axes of the slice: x: 2, y: 2, z: 4, core: 2. Of those that a mesh axis runs over, the one named last changes fastest.
Arguments:
- estimate: float32 [256, 128, 128], P('brick', 'view'), may hold values from 0.5 to 2
- views_data: float32 [2, 256, 128, 128], P('view', 'brick'), may hold values from 0.5 to 2
- psf_taps: float32 [2, 3, 17], P('view'), may hold values from 0.05 to 1
- view_offsets: int32 [2, 2], P('view'), may hold values from -4 to 4
- coverage: int32 [16, 2], P('brick'), may hold values from 0 to 1, as said below
Outputs:
- deconvolved: float32 [256, 128, 128], P('brick', 'view')
Inputs may be any that keep to these rules, and one draw needn't show every extreme that they name: `coverage`: every slab is covered by at least one view.
All inputs are finite; a program needn't handle non-finite values.
Results may differ from a plain program's by a relative error of at most 0.0001.
Values sent between devices are 32-bit elements; how exact they have to be, the bound alone decides.
No kernel may reach another device: no remote copies, remote signals or barrier semaphores. Data moves between devices by JAX's collectives and lax.ppermute only.
A program may use at most 64 MiB of HBM per device.

v0:
```python
import functools
import jax
import jax.numpy as jnp
from jax import lax
from jax.experimental import pallas as pl
from jax.experimental.pallas import tpu as pltpu
from jax.sharding import PartitionSpec as P

R = 8
ITERS = 4
HALO = 2 * R
F32, BF16 = jnp.float32, jnp.bfloat16
VMEM = pl.BlockSpec(memory_space=pltpu.VMEM)
SMEM = pl.BlockSpec(memory_space=pltpu.SMEM)


def parts(x):
    top = x.astype(BF16)
    return top, (x - top.astype(F32)).astype(BF16)


def dot(a, b):
    return jnp.dot(a, b, preferred_element_type=F32)


def stack3(blocks):
    split = [parts(b) for b in blocks]
    tops, rests = [s[0] for s in split], [s[1] for s in split]
    return jnp.concatenate(tops + rests + tops, axis=0)


def blur_rows_and_columns(own, side, ly, bx, mid, out, flip):
    depth, rows, width = own.shape
    views, window = bx.shape[0], rows + side.shape[1]
    for z in range(0, depth, 2):
        pair = stack3([jnp.concatenate([ref[z], ref[z + 1]], axis=1) for ref in (own, side)])
        result = dot(ly[...], pair)
        for v in range(views):
            for i in range(2):
                top, rest = parts(result[v * window : (v + 1) * window, i * width : (i + 1) * width])
                at = pl.ds((z + i) * window, window)
                mid[v, at, :width] = top
                mid[v, at, width:] = rest
    for v in range(views):
        for z in range(0, depth, 4):
            wide = dot(mid[v, pl.ds(z * window, 4 * window), :], bx[v])
            value = wide[:, :width] + wide[:, width:]
            for i in range(4):
                to = depth - 1 - z - i if flip else z + i
                out[v, to] = value[i * window : (i + 1) * window]


def tap(taps, v, k, even):
    return taps[v, lax.select(even, jnp.int32(k), jnp.int32(2 * R - k))]


def half_ratio(first, second, data, taps, v, y, even, depth):
    at = pl.ds(y, R)
    load = lambda i: first[v, i, at, :] if i < depth else second[v, i - depth, at, :]
    blurred = [None] * depth
    for k in range(2 * R + 1):
        t = tap(taps, v, k, even)
        for j in range(depth):
            term = t * load(j + k)
            blurred[j] = term if blurred[j] is None else blurred[j] + term
    return [
        jnp.where(blurred[j] > 0, data[v, j, at, :] / blurred[j], 0.0) for j in range(depth)
    ]


def near_kernel(taps, parity, own, side, own_in, side_in, data, ly, bx, blur_own, back, blur_in, mid):
    depth = own.shape[0]
    views, window = bx.shape[0], ly.shape[1] // 3
    even = parity[0] == 0
    blur_rows_and_columns(own, side, ly, bx, mid, blur_own, False)
    blur_rows_and_columns(own_in, side_in, ly, bx, mid, blur_in, True)
    for v in range(views):

        @pl.loop(0, window // R)
        def _(tile):
            y = pl.multiple_of(tile * R, R)
            ratio = half_ratio(blur_own, blur_in, data, taps, v, y, even, depth)
            total = [None] * depth
            for d in range(depth):
                t = tap(taps, v, d, even)
                for j in range(depth - d):
                    term = t * ratio[j]
                    total[j + d] = term if total[j + d] is None else total[j + d] + term
            for z in range(depth):
                back[v, z, pl.ds(y, R), :] = total[z]


def far_kernel(last, taps, parity, weight, own_out, side_out, data, blur_own, back, est, ly, bx, lyt, bxt, *rest):
    if last:
        out, blur_out, full, mid = rest
    else:
        out, edge, blur_out, full, mid = rest
    depth, rows, width = est.shape
    views, window = bx.shape[0], ly.shape[1] // 3
    even = parity[0] == 0
    blur_rows_and_columns(own_out, side_out, ly, bx, mid, blur_out, True)
    for v in range(views):

        @pl.loop(0, window // R)
        def _(tile):
            y = pl.multiple_of(tile * R, R)
            ratio = half_ratio(blur_out, blur_own, data, taps, v, y, even, depth)
            total = [back[v, z, pl.ds(y, R), :] for z in range(depth)]
            for d in range(depth):
                t = tap(taps, v, 2 * R - d, even)
                for z in range(depth - d):
                    total[z] = total[z] + t * ratio[z + d]
            for z in range(depth):
                full[v, z, pl.ds(y, R), :] = total[z]

    for z in range(0, depth, 2):
        for v in range(views):
            result = dot(lyt[v], stack3([jnp.concatenate([full[v, z], full[v, z + 1]], axis=1)]))
            for i in range(2):
                top, rest_ = parts(result[:, i * width : (i + 1) * width])
                at = pl.ds((z + i) * rows, rows)
                mid[v, at, :width] = top
                mid[v, at, width:] = rest_
    for z in range(0, depth, 4):
        factor = None
        total = None
        for v in range(views):
            wide = dot(mid[v, pl.ds(z * rows, 4 * rows), :], bxt[v])
            value = wide[:, :width] + wide[:, width:]
            w = weight[v]
            if views == 2:
                power = jnp.where(w == 1.0, value, jnp.where(w == 0.0, 1.0, jnp.sqrt(value)))
                factor = power if factor is None else factor * power
            else:
                term = w * jnp.log(value)
                total = term if total is None else total + term
        if factor is None:
            factor = jnp.exp(total)
        for i in range(4):
            new = est[z + i] * factor[i * rows : (i + 1) * rows]
            if last:
                out[lax.select(even, jnp.int32(z + i), jnp.int32(depth - 1 - z - i))] = new
            else:
                out[z + i] = new
                edge[z + i] = jnp.where(parity[1] == 0, new[rows - HALO :], new[:HALO])


def near(taps, parity, own, side, own_in, side_in, data, ly, bx):
    depth, rows, width = own.shape
    views, window = bx.shape[0], rows + side.shape[1]
    shape = (views, depth, window, width)
    size = views * depth * window * width
    return pl.pallas_call(
        near_kernel,
        out_shape=[jax.ShapeDtypeStruct(shape, F32)] * 2,
        in_specs=[SMEM] * 2 + [VMEM] * 7,
        out_specs=[VMEM] * 2,
        scratch_shapes=[pltpu.VMEM(shape, F32), pltpu.VMEM((views, depth * window, 2 * width), BF16)],
        compiler_params=pltpu.CompilerParams(vmem_limit_bytes=(24 if views == 2 else 48) << 20),
        cost_estimate=pl.CostEstimate(flops=size * 4000, bytes_accessed=size * 16, transcendentals=0),
        name="near",
    )(taps, parity, own, side, own_in, side_in, data, ly, bx)


def far(last, taps, parity, weight, own_out, side_out, data, blur_own, back, est, ly, bx, lyt, bxt):
    depth, rows, width = est.shape
    views, window = bx.shape[0], rows + side_out.shape[1]
    shape = (views, depth, window, width)
    size = views * depth * window * width
    outs = [jax.ShapeDtypeStruct(est.shape, F32)]
    if not last:
        outs.append(jax.ShapeDtypeStruct((depth, HALO, width), F32))
    return pl.pallas_call(
        functools.partial(far_kernel, last),
        out_shape=outs,
        in_specs=[SMEM] * 3 + [VMEM] * 10,
        out_specs=[VMEM] * len(outs),
        scratch_shapes=[pltpu.VMEM(shape, F32)] * 2 + [pltpu.VMEM((views, depth * window, 2 * width), BF16)],
        compiler_params=pltpu.CompilerParams(vmem_limit_bytes=(24 if views == 2 else 48) << 20),
        cost_estimate=pl.CostEstimate(flops=size * 4000, bytes_accessed=size * 16, transcendentals=0),
        name="far",
    )(taps, parity, weight, own_out, side_out, data, blur_own, back, est, ly, bx, lyt, bxt)


def band_kernel(taps, shifts, place, ly, lyt, bx, bxt):
    views, rows, triple = lyt.shape
    window, width = triple // 3, bx.shape[1] // 2
    low = place[2]
    iota = lambda shape, dim: lax.broadcasted_iota(jnp.int32, shape, dim)

    def position(c):
        return jnp.where(c < rows, c, jnp.where(c < rows + low, c - rows - HALO, c - low))

    def values(v, d, index):
        total = jnp.zeros(index.shape, F32)
        for k in range(2 * R + 1):
            total = jnp.where(index == k, taps[v, d * (2 * R + 1) + k], total)
        return total

    def split(value):
        top = value.astype(BF16).astype(F32)
        return top, value - top

    for v in range(views):
        for out, height, mirror in ((ly, window, False), (lyt, rows, True)):
            col = iota((height, triple), 1)
            folded = position(
                jnp.where(col < window, col, jnp.where(col < 2 * window, col - window, col - 2 * window))
            )
            line = position(iota((height, triple), 0))
            index = (line - folded if mirror else folded - line) + shifts[v, 0] + R
            top, rest = split(values(v, 1, index))
            both = jnp.where(col < 2 * window, top, rest).astype(BF16)
            if mirror:
                out[v] = both
            else:
                out[pl.ds(v * window, window), :] = both
        step = iota((width, width), 1) - iota((width, width), 0)
        for out, index in ((bx, -step), (bxt, step)):
            top, rest = split(values(v, 2, index + shifts[v, 1] + R))
            for i in range(2):
                at = pl.ds(i * width, width)
                out[v, at, :width] = top.astype(BF16)
                out[v, at, width:] = rest.astype(BF16)


def make_bands(taps, shifts, place, rows, window, width):
    views = taps.shape[0]
    shapes = [
        (views * window, 3 * window),
        (views, rows, 3 * window),
        (views, 2 * width, 2 * width),
        (views, 2 * width, 2 * width),
    ]
    return pl.pallas_call(
        band_kernel,
        out_shape=[jax.ShapeDtypeStruct(s, BF16) for s in shapes],
        in_specs=[SMEM] * 3,
        out_specs=[VMEM] * 4,
        compiler_params=pltpu.CompilerParams(vmem_limit_bytes=8 << 20),
        cost_estimate=pl.CostEstimate(flops=views * 10**8, bytes_accessed=views * 10**6, transcendentals=0),
        name="bands",
    )(taps, shifts, place)


def pair_lists(count):
    inner = [(i, i + 1) for i in range(0, count - 1, 2)]
    outer = [(i, i + 1) for i in range(1, count - 1, 2)]
    both = lambda pairs: [p for a, b in pairs for p in ((a, b), (b, a))]
    return both(inner), both(outer)


def diagonal(pairs):
    return [(2 * a + v, 2 * b + 1 - v) for a, b in pairs for v in range(2)]


def facing(block, even):
    return jnp.where(even, block, block[::-1])


def two_view_plan(estimate, views_data, taps, view_offsets, even, inner, outer):
    first = lax.axis_index("view") == 0
    swap = [(0, 1), (1, 0)]
    rows, total = estimate.shape[1], views_data.shape[2]

    def halo(current, edge):
        side = lax.ppermute(edge, "view", swap)
        outer_z = lax.ppermute(current, "brick", outer)
        outer_side = lax.ppermute(edge, ("brick", "view"), diagonal(outer))
        inner_z = lax.ppermute(current, "brick", inner)
        inner_side = lax.ppermute(side, "brick", inner)
        return side, inner_z, inner_side, outer_z, outer_side

    current = facing(estimate, even)
    edge = lax.dynamic_slice_in_dim(current, jnp.where(first, rows - HALO, 0), HALO, axis=1)

    small = jnp.concatenate([taps[0], view_offsets[0].astype(F32)])
    both = jnp.stack([small, lax.ppermute(small, "view", swap)])
    all_taps = both[:, : taps.shape[1]]
    shifts = jnp.round(both[:, taps.shape[1] :]).astype(jnp.int32)

    recorded = views_data[0]

    def window(at):
        own = lax.dynamic_slice_in_dim(recorded, at * rows, rows, axis=1)
        start = jnp.where(at == 0, rows, total - rows - HALO)
        beside = lax.dynamic_slice_in_dim(recorded, start, HALO, axis=1)
        return facing(jnp.concatenate([own, beside], axis=1), even)

    view = lax.axis_index("view")
    mine, theirs = window(view), window(1 - view)
    other = lax.ppermute(theirs, "view", swap)
    mine_far = lax.ppermute(mine[:R], "brick", outer)
    other_far = lax.ppermute(theirs[:R], ("brick", "view"), diagonal(outer))
    mine_near = lax.ppermute(mine[-R:], "brick", inner)
    other_near = lax.ppermute(other[-R:], "brick", inner)
    near_data = jnp.stack(
        [
            jnp.concatenate([mine[-R:], mine_near[::-1]]),
            jnp.concatenate([other[-R:], other_near[::-1]]),
        ]
    )
    far_data = jnp.stack(
        [
            jnp.concatenate([mine_far[::-1], mine[:R]]),
            jnp.concatenate([other_far[::-1], other[:R]]),
        ]
    )
    low = jnp.where(first, 0, HALO)
    return current, edge, all_taps, shifts, near_data, far_data, halo, low, rows + HALO


def many_view_plan(estimate, views_data, taps, view_offsets, even, inner, outer):
    rows = estimate.shape[1]
    up = [(i, i + 1) for i in range(lax.axis_size("view") - 1)]
    down = [(b, a) for a, b in up]

    def beside(block, dim):
        low = lax.slice_in_dim(block, rows - HALO, rows, axis=dim)
        high = lax.slice_in_dim(block, 0, HALO, axis=dim)
        return jnp.concatenate(
            [lax.ppermute(low, "view", up), lax.ppermute(high, "view", down)], axis=dim
        )

    def halo(current, _):
        inner_z = lax.ppermute(current, "brick", inner)
        outer_z = lax.ppermute(current, "brick", outer)
        return beside(current, 1), inner_z, beside(inner_z, 1), outer_z, beside(outer_z, 1)

    all_taps = lax.all_gather(taps, "view", axis=0, tiled=True)
    shifts = lax.all_gather(view_offsets, "view", axis=0, tiled=True)
    data = lax.all_to_all(views_data, "view", split_axis=2, concat_axis=0, tiled=True)
    data = jnp.where(even, data, data[:, ::-1])
    data = jnp.concatenate([data, beside(data, 2)], axis=2)
    inner_data = lax.ppermute(data[:, -R:], "brick", inner)[:, ::-1]
    outer_data = lax.ppermute(data[:, :R], "brick", outer)[:, ::-1]
    near_data = jnp.concatenate([data[:, -R:], inner_data], axis=1)
    far_data = jnp.concatenate([outer_data, data[:, :R]], axis=1)
    current = facing(estimate, even)
    return current, None, all_taps, shifts, near_data, far_data, halo, HALO, rows + 2 * HALO


def shards(estimate, views_data, psf_taps, view_offsets, coverage):
    brick, view = lax.axis_index("brick"), lax.axis_index("view")
    depth, rows, width = estimate.shape
    inner, outer = pair_lists(lax.axis_size("brick"))
    even = lax.rem(brick, 2) == 0
    taps = psf_taps / jnp.sum(psf_taps, axis=-1, keepdims=True)
    taps = taps.reshape(1, -1)
    pair = lax.axis_size("view") == 2
    plan = two_view_plan if pair else many_view_plan
    current, edge, taps, shifts, near_data, far_data, halo, low, window = plan(
        estimate, views_data, taps, view_offsets, even, inner, outer
    )
    cover = coverage[0].astype(F32)
    if pair:
        cover = jnp.where(view == 0, cover, cover[::-1])
    weight = cover / jnp.sum(cover)
    place = jnp.stack([lax.rem(brick, 2), view, low]).astype(jnp.int32)
    ly, lyt, bx, bxt = make_bands(taps, shifts, place, rows, window, width)
    for step in range(ITERS):
        last = step == ITERS - 1
        side, inner_z, inner_side, outer_z, outer_side = halo(current, edge)
        blur_own, back = near(
            taps, place, current, side, inner_z, inner_side, near_data, ly, bx
        )
        results = far(
            last, taps, place, weight, outer_z, outer_side, far_data, blur_own, back, current, ly, bx, lyt, bxt
        )
        current = results[0]
        edge = None if last else results[1]
    return current


def solution(mesh):
    return jax.shard_map(
        shards,
        mesh=mesh,
        in_specs=(
            P("brick", "view", None),
            P("view", "brick", None, None),
            P("view", None, None),
            P("view", None),
            P("brick", None),
        ),
        out_specs=P("brick", "view", None),
        check_vma=False,
    )
```

profile of v0, /device:TPU:17, one launch (start us, length us, event | category | flops | bytes accessed | tf_op | source)
XLA Modules:
  0.0 126.1 jit_solution(10388383064856265248)
XLA Ops:
  0.0 1.4 %reverse_select_fusion.2.own.est = f32[16,64,128]{2,1,0:T(8,128)S(1)} fusion(f32[16,64,128]{2,1,0:T(8,128)} %param.5, pred[]{:T(512)S(6)} %eq.12), kind=kLoop, calls=%fused_computation.4 | loop fusion | flops 131072 | bytes 1048577 | tf_op jit(solution)/shard_map/jit(_where)/select_n | solution.py:258
  2.1 1.2 collective-permute-start.6
  3.3 3.9 %collective-permute-start.2 = (f32[16,16,128]{2,1,0:T(8,128)}, f32[16,16,128]{2,1,0:T(8,128)S(1)}, u32[]{:S(2)}, u32[]{:S(2)}) collective-permute-start(f32[16,16,128]{2,1,0:T(8,128)} %constant_dynamic-slice_fusion), channel_id=1, source_target_pairs={{2,5},{3,4},{4,3},{5,2},{6,9},{7,8},{8,7},{9,6},{10,13},{11,12},{1... | collective-permute-start | bytes 393224 | tf_op jit(solution)/shard_map/ppermute | solution.py:269
  7.6 1.2 collective-permute-start
  11.3 0.8 slice.32
  12.4 3.2 %collective-permute-start.3 = (f32[8,80,128]{2,1,0:T(8,128)S(1)}, f32[8,80,128]{2,1,0:T(8,128)}, u32[]{:S(2)}, u32[]{:S(2)}) collective-permute-start(f32[8,80,128]{2,1,0:T(8,128)S(1)} %get-tuple-element.46), channel_id=1, source_target_pairs={{2,4},{4,2},{6,8},{8,6},{10,12},{12,10},{14,16},{16,14},{18,20},{2... | collective-permute-start | bytes 983048 | tf_op jit(solution)/shard_map/ppermute | solution.py:293
  15.7 1.4 %bands.1 = (bf16[160,240]{1,0:T(8,128)(2,1)S(1)}, bf16[2,64,240]{2,1,0:T(8,128)(2,1)S(1)}, bf16[2,256,256]{2,1,0:T(8,128)(2,1)S(1)}, bf16[2,256,256]{2,1,0:T(8,128)(2,1)S(1)}) custom-call(f32[2,51]{1,0:T(2,128)S(1)} %bitcast.33, s32[2,2]{1,0:T(2,128)S(1)} %round-nearest-even_convert_fusion.shifts, s32[3]{0:T(128)S(1)} %pad_add_fusion.place.parity), custom_call_target="tpu_custom_call" | custom-call | flops 200000000 | bytes 2000000 | tf_op jit(solution)/shard_map/bands/pallas_call | solution.py:235
  17.2 7.5 %collective-permute-done.3 = f32[8,80,128]{2,1,0:T(8,128)} collective-permute-done((f32[8,80,128]{2,1,0:T(8,128)S(1)}, f32[8,80,128]{2,1,0:T(8,128)}, u32[]{:S(2)}, u32[]{:S(2)}) %collective-permute-start.3) | collective-permute-done | bytes 327712 | tf_op jit(solution)/shard_map/ppermute | solution.py:293
  24.7 3.9 %collective-permute-start.4 = (f32[8,80,128]{2,1,0:T(8,128)}, f32[8,80,128]{2,1,0:T(8,128)}, u32[]{:S(2)}, u32[]{:S(2)}) collective-permute-start(f32[8,80,128]{2,1,0:T(8,128)} %slice.32), channel_id=1, source_target_pairs={{2,5},{3,4},{4,3},{5,2},{6,9},{7,8},{8,7},{9,6},{10,13},{11,12},{1... | collective-permute-start | bytes 983048 | tf_op jit(solution)/shard_map/ppermute | solution.py:294
  28.6 1.0 rev.27
  29.6 0.9 maximum_bitcast_fusion.2
  30.5 1.8 %fusion.2 = (f32[8,80,128]{2,1,0:T(8,128)}, f32[8,80,128]{2,1,0:T(8,128)S(1)}) fusion(f32[16,80,128]{2,1,0:T(8,128)} %collective-permute-done.5), kind=kLoop, calls=%fused_computation.27 | loop fusion | bytes 1310720 | tf_op jit(solution)/shard_map/slice | solution.py:300
  32.3 0.9 maximum_bitcast_fusion
  33.2 2.2 %collective-permute-start.1 = (f32[16,64,128]{2,1,0:T(8,128)S(1)}, f32[16,64,128]{2,1,0:T(8,128)S(1)}, u32[]{:S(2)}, u32[]{:S(2)}) collective-permute-start(f32[16,64,128]{2,1,0:T(8,128)S(1)} %reverse_select_fusion.2.own.est), channel_id=1, source_target_pairs={{2,4},{4,2},{6,8},{8,6},{10,12},{12,10},{14,16},{16,14},{18,20},{2... | collective-permute-start | bytes 1572872 | tf_op jit(solution)/shard_map/ppermute | solution.py:268
  35.9 1.0 rev.29
  36.9 1.0 copy-done.1
  38.1 1.7 %rev.31 = f32[8,80,128]{2,1,0:T(8,128)} reverse(f32[8,80,128]{2,1,0:T(8,128)} %collective-permute-done.10), dimensions={0} | reverse | bytes 655360 | tf_op jit(solution)/shard_map/rev | solution.py:300
  39.8 1.2 maximum_bitcast_fusion.3
  41.2 5.1 %near.4 = (f32[2,16,80,128]{3,2,1,0:T(8,128)S(1)}, f32[2,16,80,128]{3,2,1,0:T(8,128)S(1)}) custom-call(f32[2,51]{1,0:T(2,128)S(1)} %bitcast.34, s32[3]{0:T(128)S(1)} %pad_add_fusion.place.parity, f32[16,64,128]{2,1,0:T(8,128)S(1)} %reverse_select_fusion.2.own.est, f32[16,16,128]{2,1,0:T(8,128)S(1)} %collective-permute-done.6.side, ...), custom_call_target="tpu_custom_call" | custom-call | flops 1310720000 | bytes 5242880 | tf_op jit(solution)/shard_map/near/pallas_call | solution.py:153
  46.3 3.0 %collective-permute-done.1.own_out = f32[16,64,128]{2,1,0:T(8,128)S(1)} collective-permute-done((f32[16,64,128]{2,1,0:T(8,128)S(1)}, f32[16,64,128]{2,1,0:T(8,128)S(1)}, u32[]{:S(2)}, u32[]{:S(2)}) %collective-permute-start.1) | collective-permute-done | bytes 524320 | tf_op jit(solution)/shard_map/ppermute | solution.py:268
  49.3 4.7 %far.4 = (f32[16,64,128]{2,1,0:T(8,128)S(1)}, f32[16,16,128]{2,1,0:T(8,128)S(1)}) custom-call(f32[2,51]{1,0:T(2,128)S(1)} %bitcast.35, s32[3]{0:T(128)S(1)} %pad_add_fusion.place.parity, f32[2]{0:T(128)S(1)} %broadcast_divide_fusion.weight, f32[16,64,128]{2,1,0:T(8,128)S(1)} %collective-permute-done.1.own_out, ...), custom_call_target="tpu_custom_call" | custom-call | flops 1310720000 | bytes 5242880 | tf_op jit(solution)/shard_map/far/pallas_call | solution.py:173
  54.1 2.2 %collective-permute-start.11 = (f32[16,64,128]{2,1,0:T(8,128)S(1)}, f32[16,64,128]{2,1,0:T(8,128)S(1)}, u32[]{:S(2)}, u32[]{:S(2)}) collective-permute-start(f32[16,64,128]{2,1,0:T(8,128)S(1)} %get-tuple-element.29.own.est), channel_id=1, source_target_pairs={{2,4},{4,2},{6,8},{8,6},{10,12},{12,10},{14,16},{16,14},{18,20},{2... | collective-permute-start | bytes 1572872 | tf_op jit(solution)/shard_map/ppermute | solution.py:268
  56.4 0.7 collective-permute-start.13
  57.1 4.0 %collective-permute-done.13.side = f32[16,16,128]{2,1,0:T(8,128)S(1)} collective-permute-done((f32[16,16,128]{2,1,0:T(8,128)S(1)}, f32[16,16,128]{2,1,0:T(8,128)S(1)}, u32[]{:S(2)}, u32[]{:S(2)}) %collective-permute-start.13) | collective-permute-done | bytes 131104 | tf_op jit(solution)/shard_map/ppermute | solution.py:267
  61.1 1.2 collective-permute-start.15
  62.3 2.9 %collective-permute-start.12 = (f32[16,16,128]{2,1,0:T(8,128)S(1)}, f32[16,16,128]{2,1,0:T(8,128)S(1)}, u32[]{:S(2)}, u32[]{:S(2)}) collective-permute-start(f32[16,16,128]{2,1,0:T(8,128)S(1)} %get-tuple-element.30), channel_id=1, source_target_pairs={{2,5},{3,4},{4,3},{5,2},{6,9},{7,8},{8,7},{9,6},{10,13},{11,12},{1... | collective-permute-start | bytes 393224 | tf_op jit(solution)/shard_map/ppermute | solution.py:269
  65.3 4.6 %near.5 = (f32[2,16,80,128]{3,2,1,0:T(8,128)S(1)}, f32[2,16,80,128]{3,2,1,0:T(8,128)S(1)}) custom-call(f32[2,51]{1,0:T(2,128)S(1)} %bitcast.36, s32[3]{0:T(128)S(1)} %pad_add_fusion.place.parity, f32[16,64,128]{2,1,0:T(8,128)S(1)} %get-tuple-element.29.own.est, f32[16,16,128]{2,1,0:T(8,128)S(1)} %collective-permute-done.13.side, ...), custom_call_target="tpu_custom_call" | custom-call | flops 1310720000 | bytes 5242880 | tf_op jit(solution)/shard_map/near/pallas_call | solution.py:153
  69.9 1.1 collective-permute-done.12.side_out
  71.0 2.0 %collective-permute-done.11.own_out = f32[16,64,128]{2,1,0:T(8,128)S(1)} collective-permute-done((f32[16,64,128]{2,1,0:T(8,128)S(1)}, f32[16,64,128]{2,1,0:T(8,128)S(1)}, u32[]{:S(2)}, u32[]{:S(2)}) %collective-permute-start.11) | collective-permute-done | bytes 524320 | tf_op jit(solution)/shard_map/ppermute | solution.py:268
  73.1 4.7 %far.5 = (f32[16,64,128]{2,1,0:T(8,128)S(1)}, f32[16,16,128]{2,1,0:T(8,128)S(1)}) custom-call(f32[2,51]{1,0:T(2,128)S(1)} %bitcast.37, s32[3]{0:T(128)S(1)} %pad_add_fusion.place.parity, f32[2]{0:T(128)S(1)} %broadcast_divide_fusion.weight, f32[16,64,128]{2,1,0:T(8,128)S(1)} %collective-permute-done.11.own_out, ...), custom_call_target="tpu_custom_call" | custom-call | flops 1310720000 | bytes 5242880 | tf_op jit(solution)/shard_map/far/pallas_call | solution.py:173
  77.9 2.2 %collective-permute-start.16 = (f32[16,64,128]{2,1,0:T(8,128)S(1)}, f32[16,64,128]{2,1,0:T(8,128)S(1)}, u32[]{:S(2)}, u32[]{:S(2)}) collective-permute-start(f32[16,64,128]{2,1,0:T(8,128)S(1)} %get-tuple-element.33.own.est), channel_id=1, source_target_pairs={{2,4},{4,2},{6,8},{8,6},{10,12},{12,10},{14,16},{16,14},{18,20},{2... | collective-permute-start | bytes 1572872 | tf_op jit(solution)/shard_map/ppermute | solution.py:268
  80.1 0.7 collective-permute-start.18
  80.8 4.0 %collective-permute-done.18.side = f32[16,16,128]{2,1,0:T(8,128)S(1)} collective-permute-done((f32[16,16,128]{2,1,0:T(8,128)S(1)}, f32[16,16,128]{2,1,0:T(8,128)S(1)}, u32[]{:S(2)}, u32[]{:S(2)}) %collective-permute-start.18) | collective-permute-done | bytes 131104 | tf_op jit(solution)/shard_map/ppermute | solution.py:267
  84.9 1.2 collective-permute-start.20
  86.1 3.1 %collective-permute-start.17 = (f32[16,16,128]{2,1,0:T(8,128)S(1)}, f32[16,16,128]{2,1,0:T(8,128)S(1)}, u32[]{:S(2)}, u32[]{:S(2)}) collective-permute-start(f32[16,16,128]{2,1,0:T(8,128)S(1)} %get-tuple-element.34), channel_id=1, source_target_pairs={{2,5},{3,4},{4,3},{5,2},{6,9},{7,8},{8,7},{9,6},{10,13},{11,12},{1... | collective-permute-start | bytes 393224 | tf_op jit(solution)/shard_map/ppermute | solution.py:269
  89.2 4.6 %near.6 = (f32[2,16,80,128]{3,2,1,0:T(8,128)S(1)}, f32[2,16,80,128]{3,2,1,0:T(8,128)S(1)}) custom-call(f32[2,51]{1,0:T(2,128)S(1)} %bitcast.38, s32[3]{0:T(128)S(1)} %pad_add_fusion.place.parity, f32[16,64,128]{2,1,0:T(8,128)S(1)} %get-tuple-element.33.own.est, f32[16,16,128]{2,1,0:T(8,128)S(1)} %collective-permute-done.18.side, ...), custom_call_target="tpu_custom_call" | custom-call | flops 1310720000 | bytes 5242880 | tf_op jit(solution)/shard_map/near/pallas_call | solution.py:153
  93.9 0.9 collective-permute-done.17.side_out
  94.8 2.0 %collective-permute-done.16.own_out = f32[16,64,128]{2,1,0:T(8,128)S(1)} collective-permute-done((f32[16,64,128]{2,1,0:T(8,128)S(1)}, f32[16,64,128]{2,1,0:T(8,128)S(1)}, u32[]{:S(2)}, u32[]{:S(2)}) %collective-permute-start.16) | collective-permute-done | bytes 524320 | tf_op jit(solution)/shard_map/ppermute | solution.py:268
  96.8 4.7 %far.6 = (f32[16,64,128]{2,1,0:T(8,128)S(1)}, f32[16,16,128]{2,1,0:T(8,128)S(1)}) custom-call(f32[2,51]{1,0:T(2,128)S(1)} %bitcast.39, s32[3]{0:T(128)S(1)} %pad_add_fusion.place.parity, f32[2]{0:T(128)S(1)} %broadcast_divide_fusion.weight, f32[16,64,128]{2,1,0:T(8,128)S(1)} %collective-permute-done.16.own_out, ...), custom_call_target="tpu_custom_call" | custom-call | flops 1310720000 | bytes 5242880 | tf_op jit(solution)/shard_map/far/pallas_call | solution.py:173
  101.6 2.2 %collective-permute-start.21 = (f32[16,64,128]{2,1,0:T(8,128)S(1)}, f32[16,64,128]{2,1,0:T(8,128)S(1)}, u32[]{:S(2)}, u32[]{:S(2)}) collective-permute-start(f32[16,64,128]{2,1,0:T(8,128)S(1)} %get-tuple-element.37.own.est), channel_id=1, source_target_pairs={{2,4},{4,2},{6,8},{8,6},{10,12},{12,10},{14,16},{16,14},{18,20},{2... | collective-permute-start | bytes 1572872 | tf_op jit(solution)/shard_map/ppermute | solution.py:268
  103.8 0.7 collective-permute-start.23
  104.6 4.0 %collective-permute-done.23.side = f32[16,16,128]{2,1,0:T(8,128)S(1)} collective-permute-done((f32[16,16,128]{2,1,0:T(8,128)S(1)}, f32[16,16,128]{2,1,0:T(8,128)S(1)}, u32[]{:S(2)}, u32[]{:S(2)}) %collective-permute-start.23) | collective-permute-done | bytes 131104 | tf_op jit(solution)/shard_map/ppermute | solution.py:267
  108.6 1.2 collective-permute-start.25
  109.8 2.9 %collective-permute-start.22 = (f32[16,16,128]{2,1,0:T(8,128)S(1)}, f32[16,16,128]{2,1,0:T(8,128)S(1)}, u32[]{:S(2)}, u32[]{:S(2)}) collective-permute-start(f32[16,16,128]{2,1,0:T(8,128)S(1)} %get-tuple-element.38), channel_id=1, source_target_pairs={{2,5},{3,4},{4,3},{5,2},{6,9},{7,8},{8,7},{9,6},{10,13},{11,12},{1... | collective-permute-start | bytes 393224 | tf_op jit(solution)/shard_map/ppermute | solution.py:269
  112.8 4.6 %near.7 = (f32[2,16,80,128]{3,2,1,0:T(8,128)S(1)}, f32[2,16,80,128]{3,2,1,0:T(8,128)S(1)}) custom-call(f32[2,51]{1,0:T(2,128)S(1)} %bitcast.40, s32[3]{0:T(128)S(1)} %pad_add_fusion.place.parity, f32[16,64,128]{2,1,0:T(8,128)S(1)} %get-tuple-element.37.own.est, f32[16,16,128]{2,1,0:T(8,128)S(1)} %collective-permute-done.23.side, ...), custom_call_target="tpu_custom_call" | custom-call | flops 1310720000 | bytes 5242880 | tf_op jit(solution)/shard_map/near/pallas_call | solution.py:153
  117.4 1.1 collective-permute-done.22.side_out
  118.5 2.0 %collective-permute-done.21.own_out = f32[16,64,128]{2,1,0:T(8,128)S(1)} collective-permute-done((f32[16,64,128]{2,1,0:T(8,128)S(1)}, f32[16,64,128]{2,1,0:T(8,128)S(1)}, u32[]{:S(2)}, u32[]{:S(2)}) %collective-permute-start.21) | collective-permute-done | bytes 524320 | tf_op jit(solution)/shard_map/ppermute | solution.py:268
  120.5 5.5 %far.7 = f32[16,64,128]{2,1,0:T(8,128)} custom-call(f32[2,51]{1,0:T(2,128)S(1)} %bitcast.41, s32[3]{0:T(128)S(1)} %pad_add_fusion.place.parity, f32[2]{0:T(128)S(1)} %broadcast_divide_fusion.weight, f32[16,64,128]{2,1,0:T(8,128)S(1)} %collective-permute-done.21.own_out, f32[16,16,128]{2,1,0:T(8,128)S(1)} %collective-permute-done.22.side_out, ...), custom_call_target="tpu_custom_call" | custom-call | flops 1310720000 | bytes 5242880 | tf_op jit(solution)/shard_map/far/pallas_call | solution.py:173
  (59 shorter events, 5.0 us)
Async XLA Ops:
  0.0 7.2 %copy-start.5 = (s32[1,2]{1,0:T(1,128)S(1)}, s32[1,2]{1,0:T(1,128)}, u32[]{:S(2)}) copy-start(s32[1,2]{1,0:T(1,128)} %param.8) | copy-start | bytes 28
  0.0 7.3 %copy-start.3 = (f32[1,3,17]{2,0,1:T(1,128)S(1)}, f32[1,3,17]{2,0,1:T(1,128)}, u32[]{:S(2)}) copy-start(f32[1,3,17]{2,0,1:T(1,128)} %param.7) | copy-start | bytes 616
  0.0 8.9 %copy-start.2 = (f32[1,16,128,128]{3,2,1,0:T(8,128)S(1)}, f32[1,16,128,128]{3,2,1,0:T(8,128)}, u32[]{:S(2)}) copy-start(f32[1,16,128,128]{3,2,1,0:T(8,128)} %param.6) | copy-start | bytes 3145732
  2.1 31.1 %collective-permute-start.6 = (f32[16,16,128]{2,1,0:T(8,128)}, f32[16,16,128]{2,1,0:T(8,128)S(1)}, u32[]{:S(2)}, u32[]{:S(2)}) collective-permute-start(f32[16,16,128]{2,1,0:T(8,128)} %constant_dynamic-slice_fusion), channel_id=1, source_target_pairs={{0,1},{1,0},{2,3},{3,2},{4,5},{5,4},{6,7},{7,6},{8,9},{9,8},{10,11... | collective-permute-start | bytes 393224 | tf_op jit(solution)/shard_map/ppermute | solution.py:267
  3.3 43.0 %collective-permute-start.2 = (f32[16,16,128]{2,1,0:T(8,128)}, f32[16,16,128]{2,1,0:T(8,128)S(1)}, u32[]{:S(2)}, u32[]{:S(2)}) collective-permute-start(f32[16,16,128]{2,1,0:T(8,128)} %constant_dynamic-slice_fusion), channel_id=1, source_target_pairs={{2,5},{3,4},{4,3},{5,2},{6,9},{7,8},{8,7},{9,6},{10,13},{11,12},{1... | collective-permute-start | bytes 393224 | tf_op jit(solution)/shard_map/ppermute | solution.py:269
  7.6 4.8 %collective-permute-start = (f32[53]{0:T(128)S(1)}, f32[53]{0:T(128)S(1)}, u32[]{:S(2)}, u32[]{:S(2)}) collective-permute-start(f32[53]{0:T(128)S(1)} %pad_maximum_fusion.5), channel_id=1, source_target_pairs={{0,1},{1,0},{2,3},{3,2},{4,5},{5,4},{6,7},{7,6},{8,9},{9,8},{10,11... | collective-permute-start | bytes 644 | tf_op jit(solution)/shard_map/ppermute | solution.py:278
  9.1 8.0 %collective-permute-start.9 = (f32[8,80,128]{2,1,0:T(8,128)S(1)}, f32[8,80,128]{2,1,0:T(8,128)S(1)}, u32[]{:S(2)}, u32[]{:S(2)}) collective-permute-start(f32[8,80,128]{2,1,0:T(8,128)S(1)} %get-tuple-element.45), channel_id=1, source_target_pairs={{0,2},{2,0},{4,6},{6,4},{8,10},{10,8},{12,14},{14,12},{16,18},{18,... | collective-permute-start | bytes 983048 | tf_op jit(solution)/shard_map/ppermute | solution.py:295
  9.2 0.7 copy-start.4
  9.3 21.1 %collective-permute-start.5 = (f32[16,80,128]{2,1,0:T(8,128)S(1)}, f32[16,80,128]{2,1,0:T(8,128)}, u32[]{:S(2)}, u32[]{:S(2)}) collective-permute-start(f32[16,80,128]{2,1,0:T(8,128)S(1)} %reverse_select_fusion), channel_id=1, source_target_pairs={{0,1},{1,0},{2,3},{3,2},{4,5},{5,4},{6,7},{7,6},{8,9},{9,8},{10,11... | collective-permute-start | bytes 1966088 | tf_op jit(solution)/shard_map/ppermute | solution.py:292
  12.4 12.3 %collective-permute-start.3 = (f32[8,80,128]{2,1,0:T(8,128)S(1)}, f32[8,80,128]{2,1,0:T(8,128)}, u32[]{:S(2)}, u32[]{:S(2)}) collective-permute-start(f32[8,80,128]{2,1,0:T(8,128)S(1)} %get-tuple-element.46), channel_id=1, source_target_pairs={{2,4},{4,2},{6,8},{8,6},{10,12},{12,10},{14,16},{16,14},{18,20},{2... | collective-permute-start | bytes 983048 | tf_op jit(solution)/shard_map/ppermute | solution.py:293
  17.1 24.1 %collective-permute-start.7 = (f32[16,64,128]{2,1,0:T(8,128)S(1)}, f32[16,64,128]{2,1,0:T(8,128)}, u32[]{:S(2)}, u32[]{:S(2)}) collective-permute-start(f32[16,64,128]{2,1,0:T(8,128)S(1)} %reverse_select_fusion.2.own.est), channel_id=1, source_target_pairs={{0,2},{2,0},{4,6},{6,4},{8,10},{10,8},{12,14},{14,12},{16,18},{18,... | collective-permute-start | bytes 1572872 | tf_op jit(solution)/shard_map/ppermute | solution.py:270
  24.7 10.7 %collective-permute-start.4 = (f32[8,80,128]{2,1,0:T(8,128)}, f32[8,80,128]{2,1,0:T(8,128)}, u32[]{:S(2)}, u32[]{:S(2)}) collective-permute-start(f32[8,80,128]{2,1,0:T(8,128)} %slice.32), channel_id=1, source_target_pairs={{2,5},{3,4},{4,3},{5,2},{6,9},{7,8},{8,7},{9,6},{10,13},{11,12},{1... | collective-permute-start | bytes 983048 | tf_op jit(solution)/shard_map/ppermute | solution.py:294
  32.3 5.7 %collective-permute-start.10 = (f32[8,80,128]{2,1,0:T(8,128)}, f32[8,80,128]{2,1,0:T(8,128)}, u32[]{:S(2)}, u32[]{:S(2)}) collective-permute-start(f32[8,80,128]{2,1,0:T(8,128)} %get-tuple-element.47), channel_id=1, source_target_pairs={{0,2},{2,0},{4,6},{6,4},{8,10},{10,8},{12,14},{14,12},{16,18},{18,... | collective-permute-start | bytes 983048 | tf_op jit(solution)/shard_map/ppermute | solution.py:296
  33.2 16.1 %collective-permute-start.1 = (f32[16,64,128]{2,1,0:T(8,128)S(1)}, f32[16,64,128]{2,1,0:T(8,128)S(1)}, u32[]{:S(2)}, u32[]{:S(2)}) collective-permute-start(f32[16,64,128]{2,1,0:T(8,128)S(1)} %reverse_select_fusion.2.own.est), channel_id=1, source_target_pairs={{2,4},{4,2},{6,8},{8,6},{10,12},{12,10},{14,16},{16,14},{18,20},{2... | collective-permute-start | bytes 1572872 | tf_op jit(solution)/shard_map/ppermute | solution.py:268
  35.4 5.7 %collective-permute-start.8 = (f32[16,16,128]{2,1,0:T(8,128)S(1)}, f32[16,16,128]{2,1,0:T(8,128)S(1)}, u32[]{:S(2)}, u32[]{:S(2)}) collective-permute-start(f32[16,16,128]{2,1,0:T(8,128)S(1)} %collective-permute-done.6.side), channel_id=1, source_target_pairs={{0,2},{2,0},{4,6},{6,4},{8,10},{10,8},{12,14},{14,12},{16,18},{18,... | collective-permute-start | bytes 393224 | tf_op jit(solution)/shard_map/ppermute | solution.py:271
  36.9 1.1 copy-start.1
  39.8 1.3 %copy-start = (f32[1,16,80,128]{3,2,1,0:T(8,128)S(1)}, f32[1,16,80,128]{3,2,1,0:T(8,128)}, u32[]{:S(2)}) copy-start(f32[1,16,80,128]{3,2,1,0:T(8,128)} %maximum_bitcast_fusion.2) | copy-start | bytes 1966084
  54.1 11.2 %collective-permute-start.14 = (f32[16,64,128]{2,1,0:T(8,128)S(1)}, f32[16,64,128]{2,1,0:T(8,128)S(1)}, u32[]{:S(2)}, u32[]{:S(2)}) collective-permute-start(f32[16,64,128]{2,1,0:T(8,128)S(1)} %get-tuple-element.29.own.est), channel_id=1, source_target_pairs={{0,2},{2,0},{4,6},{6,4},{8,10},{10,8},{12,14},{14,12},{16,18},{18,... | collective-permute-start | bytes 1572872 | tf_op jit(solution)/shard_map/ppermute | solution.py:270
  54.1 18.9 %collective-permute-start.11 = (f32[16,64,128]{2,1,0:T(8,128)S(1)}, f32[16,64,128]{2,1,0:T(8,128)S(1)}, u32[]{:S(2)}, u32[]{:S(2)}) collective-permute-start(f32[16,64,128]{2,1,0:T(8,128)S(1)} %get-tuple-element.29.own.est), channel_id=1, source_target_pairs={{2,4},{4,2},{6,8},{8,6},{10,12},{12,10},{14,16},{16,14},{18,20},{2... | collective-permute-start | bytes 1572872 | tf_op jit(solution)/shard_map/ppermute | solution.py:268
  56.4 4.7 %collective-permute-start.13 = (f32[16,16,128]{2,1,0:T(8,128)S(1)}, f32[16,16,128]{2,1,0:T(8,128)S(1)}, u32[]{:S(2)}, u32[]{:S(2)}) collective-permute-start(f32[16,16,128]{2,1,0:T(8,128)S(1)} %get-tuple-element.30), channel_id=1, source_target_pairs={{0,1},{1,0},{2,3},{3,2},{4,5},{5,4},{6,7},{7,6},{8,9},{9,8},{10,11... | collective-permute-start | bytes 393224 | tf_op jit(solution)/shard_map/ppermute | solution.py:267
  61.1 4.2 %collective-permute-start.15 = (f32[16,16,128]{2,1,0:T(8,128)S(1)}, f32[16,16,128]{2,1,0:T(8,128)S(1)}, u32[]{:S(2)}, u32[]{:S(2)}) collective-permute-start(f32[16,16,128]{2,1,0:T(8,128)S(1)} %collective-permute-done.13.side), channel_id=1, source_target_pairs={{0,2},{2,0},{4,6},{6,4},{8,10},{10,8},{12,14},{14,12},{16,18},{18,... | collective-permute-start | bytes 393224 | tf_op jit(solution)/shard_map/ppermute | solution.py:271
  62.3 8.7 %collective-permute-start.12 = (f32[16,16,128]{2,1,0:T(8,128)S(1)}, f32[16,16,128]{2,1,0:T(8,128)S(1)}, u32[]{:S(2)}, u32[]{:S(2)}) collective-permute-start(f32[16,16,128]{2,1,0:T(8,128)S(1)} %get-tuple-element.30), channel_id=1, source_target_pairs={{2,5},{3,4},{4,3},{5,2},{6,9},{7,8},{8,7},{9,6},{10,13},{11,12},{1... | collective-permute-start | bytes 393224 | tf_op jit(solution)/shard_map/ppermute | solution.py:269
  77.8 11.4 %collective-permute-start.19 = (f32[16,64,128]{2,1,0:T(8,128)S(1)}, f32[16,64,128]{2,1,0:T(8,128)S(1)}, u32[]{:S(2)}, u32[]{:S(2)}) collective-permute-start(f32[16,64,128]{2,1,0:T(8,128)S(1)} %get-tuple-element.33.own.est), channel_id=1, source_target_pairs={{0,2},{2,0},{4,6},{6,4},{8,10},{10,8},{12,14},{14,12},{16,18},{18,... | collective-permute-start | bytes 1572872 | tf_op jit(solution)/shard_map/ppermute | solution.py:270
  77.9 18.9 %collective-permute-start.16 = (f32[16,64,128]{2,1,0:T(8,128)S(1)}, f32[16,64,128]{2,1,0:T(8,128)S(1)}, u32[]{:S(2)}, u32[]{:S(2)}) collective-permute-start(f32[16,64,128]{2,1,0:T(8,128)S(1)} %get-tuple-element.33.own.est), channel_id=1, source_target_pairs={{2,4},{4,2},{6,8},{8,6},{10,12},{12,10},{14,16},{16,14},{18,20},{2... | collective-permute-start | bytes 1572872 | tf_op jit(solution)/shard_map/ppermute | solution.py:268
  80.1 4.8 %collective-permute-start.18 = (f32[16,16,128]{2,1,0:T(8,128)S(1)}, f32[16,16,128]{2,1,0:T(8,128)S(1)}, u32[]{:S(2)}, u32[]{:S(2)}) collective-permute-start(f32[16,16,128]{2,1,0:T(8,128)S(1)} %get-tuple-element.34), channel_id=1, source_target_pairs={{0,1},{1,0},{2,3},{3,2},{4,5},{5,4},{6,7},{7,6},{8,9},{9,8},{10,11... | collective-permute-start | bytes 393224 | tf_op jit(solution)/shard_map/ppermute | solution.py:267
  84.9 4.4 %collective-permute-start.20 = (f32[16,16,128]{2,1,0:T(8,128)S(1)}, f32[16,16,128]{2,1,0:T(8,128)S(1)}, u32[]{:S(2)}, u32[]{:S(2)}) collective-permute-start(f32[16,16,128]{2,1,0:T(8,128)S(1)} %collective-permute-done.18.side), channel_id=1, source_target_pairs={{0,2},{2,0},{4,6},{6,4},{8,10},{10,8},{12,14},{14,12},{16,18},{18,... | collective-permute-start | bytes 393224 | tf_op jit(solution)/shard_map/ppermute | solution.py:271
  86.1 8.7 %collective-permute-start.17 = (f32[16,16,128]{2,1,0:T(8,128)S(1)}, f32[16,16,128]{2,1,0:T(8,128)S(1)}, u32[]{:S(2)}, u32[]{:S(2)}) collective-permute-start(f32[16,16,128]{2,1,0:T(8,128)S(1)} %get-tuple-element.34), channel_id=1, source_target_pairs={{2,5},{3,4},{4,3},{5,2},{6,9},{7,8},{8,7},{9,6},{10,13},{11,12},{1... | collective-permute-start | bytes 393224 | tf_op jit(solution)/shard_map/ppermute | solution.py:269
  101.5 11.2 %collective-permute-start.24 = (f32[16,64,128]{2,1,0:T(8,128)S(1)}, f32[16,64,128]{2,1,0:T(8,128)S(1)}, u32[]{:S(2)}, u32[]{:S(2)}) collective-permute-start(f32[16,64,128]{2,1,0:T(8,128)S(1)} %get-tuple-element.37.own.est), channel_id=1, source_target_pairs={{0,2},{2,0},{4,6},{6,4},{8,10},{10,8},{12,14},{14,12},{16,18},{18,... | collective-permute-start | bytes 1572872 | tf_op jit(solution)/shard_map/ppermute | solution.py:270
  101.6 18.9 %collective-permute-start.21 = (f32[16,64,128]{2,1,0:T(8,128)S(1)}, f32[16,64,128]{2,1,0:T(8,128)S(1)}, u32[]{:S(2)}, u32[]{:S(2)}) collective-permute-start(f32[16,64,128]{2,1,0:T(8,128)S(1)} %get-tuple-element.37.own.est), channel_id=1, source_target_pairs={{2,4},{4,2},{6,8},{8,6},{10,12},{12,10},{14,16},{16,14},{18,20},{2... | collective-permute-start | bytes 1572872 | tf_op jit(solution)/shard_map/ppermute | solution.py:268
  103.8 4.8 %collective-permute-start.23 = (f32[16,16,128]{2,1,0:T(8,128)S(1)}, f32[16,16,128]{2,1,0:T(8,128)S(1)}, u32[]{:S(2)}, u32[]{:S(2)}) collective-permute-start(f32[16,16,128]{2,1,0:T(8,128)S(1)} %get-tuple-element.38), channel_id=1, source_target_pairs={{0,1},{1,0},{2,3},{3,2},{4,5},{5,4},{6,7},{7,6},{8,9},{9,8},{10,11... | collective-permute-start | bytes 393224 | tf_op jit(solution)/shard_map/ppermute | solution.py:267
  108.6 4.2 %collective-permute-start.25 = (f32[16,16,128]{2,1,0:T(8,128)S(1)}, f32[16,16,128]{2,1,0:T(8,128)S(1)}, u32[]{:S(2)}, u32[]{:S(2)}) collective-permute-start(f32[16,16,128]{2,1,0:T(8,128)S(1)} %collective-permute-done.23.side), channel_id=1, source_target_pairs={{0,2},{2,0},{4,6},{6,4},{8,10},{10,8},{12,14},{14,12},{16,18},{18,... | collective-permute-start | bytes 393224 | tf_op jit(solution)/shard_map/ppermute | solution.py:271
  109.8 8.7 %collective-permute-start.22 = (f32[16,16,128]{2,1,0:T(8,128)S(1)}, f32[16,16,128]{2,1,0:T(8,128)S(1)}, u32[]{:S(2)}, u32[]{:S(2)}) collective-permute-start(f32[16,16,128]{2,1,0:T(8,128)S(1)} %get-tuple-element.38), channel_id=1, source_target_pairs={{2,5},{3,4},{4,3},{5,2},{6,9},{7,8},{8,7},{9,6},{10,13},{11,12},{1... | collective-permute-start | bytes 393224 | tf_op jit(solution)/shard_map/ppermute | solution.py:269
where the time goes:
time: 127 us; the launch traced here: 126 us
  Pallas kernels  40.1 us (32%)
  starting transfers between devices  38.3 us (30%)
  waiting for transfers between devices  32.1 us (25%)
  local copies, waits for them, and re-layouts  8.7 us (7%)
  other arithmetic  6.42 us (5%)
    pallas_call x4, Pallas kernels, far(): pl.pallas_call(functools.partial(far_kernel, last), out_shape=outs, in_sp...  19.7 us
    pallas_call x4, Pallas kernels, near(): pl.pallas_call(near_kernel, out_shape=[jax.ShapeDtypeStruct(shape, F32)]...  19 us
    ppermute x4, starting transfers between devices, halo(): outer_side = lax.ppermute(edge, ('brick', 'view'), diagonal(outer))  12.9 us
    ppermute x4, waiting for transfers between devices, halo(): side = lax.ppermute(edge, 'view', swap)  12.1 us
    ppermute x4, waiting for transfers between devices, halo(): outer_z = lax.ppermute(current, 'brick', outer)  9.11 us
    ppermute x4, starting transfers between devices, halo(): outer_z = lax.ppermute(current, 'brick', outer)  8.85 us
    ppermute x1, waiting for transfers between devices, two_view_plan(): mine_far = lax.ppermute(mine[:R], 'brick', outer)  7.49 us
    ppermute x4, starting transfers between devices, halo(): inner_side = lax.ppermute(side, 'brick', inner)  4.13 us
  transfers between devices with their start and end apart: 26, of which 12 were waited for; matrix products, arithmetic and copies ran while one was open for 9% of the time, Pallas kernels for 16%

commit v1 on v0

--- a/solution.py
+++ b/solution.py
@@ -6,9 +6,11 @@
 from jax.experimental.pallas import tpu as pltpu
 from jax.sharding import PartitionSpec as P
 
+
 R = 8
 ITERS = 4
 HALO = 2 * R
+
 F32, BF16 = jnp.float32, jnp.bfloat16
 VMEM = pl.BlockSpec(memory_space=pltpu.VMEM)
 SMEM = pl.BlockSpec(memory_space=pltpu.SMEM)
@@ -54,23 +56,19 @@
     return taps[v, lax.select(even, jnp.int32(k), jnp.int32(2 * R - k))]
 
 
-def half_ratio(first, second, data, taps, v, y, even, depth):
-    at = pl.ds(y, R)
-    load = lambda i: first[v, i, at, :] if i < depth else second[v, i - depth, at, :]
-    blurred = [None] * depth
-    for k in range(2 * R + 1):
-        t = tap(taps, v, k, even)
-        for j in range(depth):
-            term = t * load(j + k)
-            blurred[j] = term if blurred[j] is None else blurred[j] + term
-    return [
-        jnp.where(blurred[j] > 0, data[v, j, at, :] / blurred[j], 0.0) for j in range(depth)
-    ]
-
-
-def near_kernel(taps, parity, own, side, own_in, side_in, data, ly, bx, blur_own, back, blur_in, mid):
+def ratios(seen, blurred):
+    return [jnp.where(b > 0, d / b, 0.0) for d, b in zip(seen, blurred)]
+
+
+def gather(total, at, term):
+    total[at] = term if total[at] is None else total[at] + term
+
+
+def near_kernel(views, taps, parity, own, side, own_in, side_in, ly, bx, *refs):
+    data_own, data_in = refs[:views], refs[views : 2 * views]
+    blur_far, back, blur_own, blur_in, mid = refs[2 * views :]
     depth = own.shape[0]
-    views, window = bx.shape[0], ly.shape[1] // 3
+    window = ly.shape[1] // 3
     even = parity[0] == 0
     blur_rows_and_columns(own, side, ly, bx, mid, blur_own, False)
     blur_rows_and_columns(own_in, side_in, ly, bx, mid, blur_in, True)
@@ -78,49 +76,71 @@
 
         @pl.loop(0, window // R)
         def _(tile):
-            y = pl.multiple_of(tile * R, R)
-            ratio = half_ratio(blur_own, blur_in, data, taps, v, y, even, depth)
+            at = pl.ds(pl.multiple_of(tile * R, R), R)
+            load = lambda i: blur_own[v, i, at, :] if i < depth else blur_in[v, i - depth, at, :]
+            blurred = [None] * depth
+            for k in range(2 * R + 1):
+                t = tap(taps, v, k, even)
+                for j in range(depth):
+                    gather(blurred, j, t * load(j + k))
+            seen = [data_own[v][j, at, :] for j in range(R)]
+            seen += [data_in[v][R - 1 - j, at, :] for j in range(R)]
+            ratio = ratios(seen, blurred)
             total = [None] * depth
             for d in range(depth):
                 t = tap(taps, v, d, even)
                 for j in range(depth - d):
-                    term = t * ratio[j]
-                    total[j + d] = term if total[j + d] is None else total[j + d] + term
+                    gather(total, j + d, t * ratio[j])
             for z in range(depth):
-                back[v, z, pl.ds(y, R), :] = total[z]
-
-
-def far_kernel(last, taps, parity, weight, own_out, side_out, data, blur_own, back, est, ly, bx, lyt, bxt, *rest):
-    if last:
-        out, blur_out, full, mid = rest
-    else:
-        out, edge, blur_out, full, mid = rest
+                back[v, z, at, :] = total[z]
+            partial = [None] * depth
+            for k in range(1, 2 * R + 1):
+                t = tap(taps, v, k, even)
+                for j in range(max(0, depth - k), depth):
+                    gather(partial, j, t * load(j + k - depth))
+            for j in range(depth):
+                blur_far[v, j, at, :] = (
+                    jnp.zeros_like(total[0]) if partial[j] is None else partial[j]
+                )
+
+
+def far_kernel(last, views, taps, parity, weight, own_out, side_out, blur_far, back, est, ly, bx, lyt, bxt, *refs):
+    data_out, data_own = refs[:views], refs[views : 2 * views]
+    out, edge = refs[2 * views], None if last else refs[2 * views + 1]
+    blur_out, full, mid = refs[-3:]
     depth, rows, width = est.shape
-    views, window = bx.shape[0], ly.shape[1] // 3
+    window = ly.shape[1] // 3
     even = parity[0] == 0
     blur_rows_and_columns(own_out, side_out, ly, bx, mid, blur_out, True)
     for v in range(views):
 
         @pl.loop(0, window // R)
         def _(tile):
-            y = pl.multiple_of(tile * R, R)
-            ratio = half_ratio(blur_out, blur_own, data, taps, v, y, even, depth)
-            total = [back[v, z, pl.ds(y, R), :] for z in range(depth)]
+            at = pl.ds(pl.multiple_of(tile * R, R), R)
+            blurred = [blur_far[v, j, at, :] for j in range(depth)]
+            for k in range(2 * R):
+                t = tap(taps, v, k, even)
+                for j in range(depth - k):
+                    blurred[j] = blurred[j] + t * blur_out[v, j + k, at, :]
+            seen = [data_out[v][R - 1 - j, at, :] for j in range(R)]
+            seen += [data_own[v][j, at, :] for j in range(R)]
+            ratio = ratios(seen, blurred)
+            total = [back[v, z, at, :] for z in range(depth)]
             for d in range(depth):
                 t = tap(taps, v, 2 * R - d, even)
                 for z in range(depth - d):
                     total[z] = total[z] + t * ratio[z + d]
             for z in range(depth):
-                full[v, z, pl.ds(y, R), :] = total[z]
+                full[v, z, at, :] = total[z]
 
     for z in range(0, depth, 2):
         for v in range(views):
             result = dot(lyt[v], stack3([jnp.concatenate([full[v, z], full[v, z + 1]], axis=1)]))
             for i in range(2):
-                top, rest_ = parts(result[:, i * width : (i + 1) * width])
+                top, rest = parts(result[:, i * width : (i + 1) * width])
                 at = pl.ds((z + i) * rows, rows)
                 mid[v, at, :width] = top
-                mid[v, at, width:] = rest_
+                mid[v, at, width:] = rest
     for z in range(0, depth, 4):
         factor = None
         total = None
@@ -145,24 +165,25 @@
                 edge[z + i] = jnp.where(parity[1] == 0, new[rows - HALO :], new[:HALO])
 
 
-def near(taps, parity, own, side, own_in, side_in, data, ly, bx):
+def near(taps, place, own, side, own_in, side_in, ly, bx, data_own, data_in):
     depth, rows, width = own.shape
     views, window = bx.shape[0], rows + side.shape[1]
     shape = (views, depth, window, width)
     size = views * depth * window * width
     return pl.pallas_call(
-        near_kernel,
+        functools.partial(near_kernel, views),
         out_shape=[jax.ShapeDtypeStruct(shape, F32)] * 2,
-        in_specs=[SMEM] * 2 + [VMEM] * 7,
+        in_specs=[SMEM] * 2 + [VMEM] * (6 + 2 * views),
         out_specs=[VMEM] * 2,
-        scratch_shapes=[pltpu.VMEM(shape, F32), pltpu.VMEM((views, depth * window, 2 * width), BF16)],
+        scratch_shapes=[pltpu.VMEM(shape, F32)] * 2
+        + [pltpu.VMEM((views, depth * window, 2 * width), BF16)],
         compiler_params=pltpu.CompilerParams(vmem_limit_bytes=(24 if views == 2 else 48) << 20),
         cost_estimate=pl.CostEstimate(flops=size * 4000, bytes_accessed=size * 16, transcendentals=0),
         name="near",
-    )(taps, parity, own, side, own_in, side_in, data, ly, bx)
-
-
-def far(last, taps, parity, weight, own_out, side_out, data, blur_own, back, est, ly, bx, lyt, bxt):
+    )(taps, place, own, side, own_in, side_in, ly, bx, *data_own, *data_in)
+
+
+def far(last, taps, place, weight, own_out, side_out, blur_far, back, est, ly, bx, lyt, bxt, data_out, data_own):
     depth, rows, width = est.shape
     views, window = bx.shape[0], rows + side_out.shape[1]
     shape = (views, depth, window, width)
@@ -171,15 +192,49 @@
     if not last:
         outs.append(jax.ShapeDtypeStruct((depth, HALO, width), F32))
     return pl.pallas_call(
-        functools.partial(far_kernel, last),
+        functools.partial(far_kernel, last, views),
         out_shape=outs,
-        in_specs=[SMEM] * 3 + [VMEM] * 10,
+        in_specs=[SMEM] * 3 + [VMEM] * (9 + 2 * views),
         out_specs=[VMEM] * len(outs),
-        scratch_shapes=[pltpu.VMEM(shape, F32)] * 2 + [pltpu.VMEM((views, depth * window, 2 * width), BF16)],
+        scratch_shapes=[pltpu.VMEM(shape, F32)] * 2
+        + [pltpu.VMEM((views, depth * window, 2 * width), BF16)],
         compiler_params=pltpu.CompilerParams(vmem_limit_bytes=(24 if views == 2 else 48) << 20),
         cost_estimate=pl.CostEstimate(flops=size * 4000, bytes_accessed=size * 16, transcendentals=0),
         name="far",
-    )(taps, parity, weight, own_out, side_out, data, blur_own, back, est, ly, bx, lyt, bxt)
+    )(taps, place, weight, own_out, side_out, blur_far, back, est, ly, bx, lyt, bxt, *data_out, *data_own)
+
+
+def estimate_kernel(place, estimate, out, edge):
+    depth, rows, _ = estimate.shape
+    start = pl.multiple_of(jnp.where(place[1] == 0, rows - HALO, 0), HALO)
+    for z in range(depth):
+        at = lax.select(place[0] == 0, jnp.int32(z), jnp.int32(depth - 1 - z))
+        out[z] = estimate[at]
+        edge[z] = estimate[at, pl.ds(start, HALO), :]
+
+
+def recorded_kernel(place, recorded, mine_out, mine_in, theirs_out, theirs_in):
+    _, depth, total, _ = recorded.shape
+    rows = total // 2
+    for z in range(depth):
+        at = lax.select(place[0] == 0, jnp.int32(z), jnp.int32(depth - 1 - z))
+        for view, outs in ((place[1], (mine_out, mine_in)), (1 - place[1], (theirs_out, theirs_in))):
+            out, to = (outs[0], z) if z < depth // 2 else (outs[1], z - depth // 2)
+            start = pl.multiple_of(view * rows, R)
+            out[to, :rows] = recorded[0, at, pl.ds(start, rows), :]
+            start = pl.multiple_of(jnp.where(view == 0, rows, total - rows - HALO), R)
+            out[to, rows:] = recorded[0, at, pl.ds(start, HALO), :]
+
+
+def simple_call(body, place, array, shapes):
+    return pl.pallas_call(
+        body,
+        out_shape=[jax.ShapeDtypeStruct(shape, F32) for shape in shapes],
+        in_specs=[SMEM, VMEM],
+        out_specs=[VMEM] * len(shapes),
+        compiler_params=pltpu.CompilerParams(vmem_limit_bytes=8 << 20),
+        cost_estimate=pl.CostEstimate(flops=0, bytes_accessed=8 * array.size, transcendentals=0),
+    )(place, array)
 
 
 def band_kernel(taps, shifts, place, ly, lyt, bx, bxt):
@@ -254,64 +309,45 @@
     return [(2 * a + v, 2 * b + 1 - v) for a, b in pairs for v in range(2)]
 
 
-def facing(block, even):
-    return jnp.where(even, block, block[::-1])
-
-
-def two_view_plan(estimate, views_data, taps, view_offsets, even, inner, outer):
-    first = lax.axis_index("view") == 0
+def two_view_plan(estimate, views_data, taps, view_offsets, place, inner, outer):
     swap = [(0, 1), (1, 0)]
-    rows, total = estimate.shape[1], views_data.shape[2]
+    depth, rows, width = estimate.shape
+    window = rows + HALO
+    axes = ("brick", "view")
+    first = place[1] == 0
 
     def halo(current, edge):
+        outer_z = lax.ppermute(current, "brick", outer)
+        outer_side = lax.ppermute(edge, axes, diagonal(outer))
         side = lax.ppermute(edge, "view", swap)
-        outer_z = lax.ppermute(current, "brick", outer)
-        outer_side = lax.ppermute(edge, ("brick", "view"), diagonal(outer))
         inner_z = lax.ppermute(current, "brick", inner)
-        inner_side = lax.ppermute(side, "brick", inner)
+        inner_side = lax.ppermute(edge, axes, diagonal(inner))
         return side, inner_z, inner_side, outer_z, outer_side
 
-    current = facing(estimate, even)
-    edge = lax.dynamic_slice_in_dim(current, jnp.where(first, rows - HALO, 0), HALO, axis=1)
-
+    prep = jnp.concatenate([place, jnp.where(first, 0, HALO)[None]]).astype(jnp.int32)
+    current, edge = simple_call(estimate_kernel, prep, estimate, [estimate.shape, (depth, HALO, width)])
     small = jnp.concatenate([taps[0], view_offsets[0].astype(F32)])
     both = jnp.stack([small, lax.ppermute(small, "view", swap)])
     all_taps = both[:, : taps.shape[1]]
     shifts = jnp.round(both[:, taps.shape[1] :]).astype(jnp.int32)
 
-    recorded = views_data[0]
-
-    def window(at):
-        own = lax.dynamic_slice_in_dim(recorded, at * rows, rows, axis=1)
-        start = jnp.where(at == 0, rows, total - rows - HALO)
-        beside = lax.dynamic_slice_in_dim(recorded, start, HALO, axis=1)
-        return facing(jnp.concatenate([own, beside], axis=1), even)
-
-    view = lax.axis_index("view")
-    mine, theirs = window(view), window(1 - view)
-    other = lax.ppermute(theirs, "view", swap)
-    mine_far = lax.ppermute(mine[:R], "brick", outer)
-    other_far = lax.ppermute(theirs[:R], ("brick", "view"), diagonal(outer))
-    mine_near = lax.ppermute(mine[-R:], "brick", inner)
-    other_near = lax.ppermute(other[-R:], "brick", inner)
-    near_data = jnp.stack(
-        [
-            jnp.concatenate([mine[-R:], mine_near[::-1]]),
-            jnp.concatenate([other[-R:], other_near[::-1]]),
-        ]
+    mine_out, mine_in, theirs_out, theirs_in = simple_call(
+        recorded_kernel, prep, views_data, [(depth // 2, window, width)] * 4
     )
-    far_data = jnp.stack(
-        [
-            jnp.concatenate([mine_far[::-1], mine[:R]]),
-            jnp.concatenate([other_far[::-1], other[:R]]),
-        ]
-    )
-    low = jnp.where(first, 0, HALO)
-    return current, edge, all_taps, shifts, near_data, far_data, halo, low, rows + HALO
-
-
-def many_view_plan(estimate, views_data, taps, view_offsets, even, inner, outer):
+    other_in = lax.ppermute(theirs_in, "view", swap)
+    other_out = lax.ppermute(theirs_out, "view", swap)
+    mine_far = lax.ppermute(mine_out, "brick", outer)
+    other_far = lax.ppermute(theirs_out, axes, diagonal(outer))
+    mine_near = lax.ppermute(mine_in, "brick", inner)
+    other_near = lax.ppermute(other_in, "brick", inner)
+    near_data = (mine_in, other_in), (mine_near, other_near)
+    far_data = (mine_far, other_far), (mine_out, other_out)
+    return current, edge, all_taps, shifts, near_data, far_data, halo, prep, window
+
+
+def many_view_plan(estimate, views_data, taps, view_offsets, place, inner, outer):
     rows = estimate.shape[1]
+    even = place[0] == 0
     up = [(i, i + 1) for i in range(lax.axis_size("view") - 1)]
     down = [(b, a) for a, b in up]
 
@@ -332,40 +368,41 @@
     data = lax.all_to_all(views_data, "view", split_axis=2, concat_axis=0, tiled=True)
     data = jnp.where(even, data, data[:, ::-1])
     data = jnp.concatenate([data, beside(data, 2)], axis=2)
-    inner_data = lax.ppermute(data[:, -R:], "brick", inner)[:, ::-1]
-    outer_data = lax.ppermute(data[:, :R], "brick", outer)[:, ::-1]
-    near_data = jnp.concatenate([data[:, -R:], inner_data], axis=1)
-    far_data = jnp.concatenate([outer_data, data[:, :R]], axis=1)
-    current = facing(estimate, even)
-    return current, None, all_taps, shifts, near_data, far_data, halo, HALO, rows + 2 * HALO
+    views = range(data.shape[0])
+    ends = lambda array: tuple(array[v] for v in views)
+    mine_in, mine_out = data[:, -R:], data[:, :R]
+    near_data = ends(mine_in), ends(lax.ppermute(mine_in, "brick", inner))
+    far_data = ends(lax.ppermute(mine_out, "brick", outer)), ends(mine_out)
+    current = jnp.where(even, estimate, estimate[::-1])
+    place = jnp.concatenate([place, jnp.full((1,), HALO, place.dtype)])
+    return current, None, all_taps, shifts, near_data, far_data, halo, place, rows + 2 * HALO
 
 
 def shards(estimate, views_data, psf_taps, view_offsets, coverage):
     brick, view = lax.axis_index("brick"), lax.axis_index("view")
-    depth, rows, width = estimate.shape
+    _, rows, width = estimate.shape
     inner, outer = pair_lists(lax.axis_size("brick"))
-    even = lax.rem(brick, 2) == 0
+    pair = lax.axis_size("view") == 2
+    plan = two_view_plan if pair else many_view_plan
     taps = psf_taps / jnp.sum(psf_taps, axis=-1, keepdims=True)
     taps = taps.reshape(1, -1)
-    pair = lax.axis_size("view") == 2
-    plan = two_view_plan if pair else many_view_plan
-    current, edge, taps, shifts, near_data, far_data, halo, low, window = plan(
-        estimate, views_data, taps, view_offsets, even, inner, outer
+    place = jnp.stack([lax.rem(brick, 2), view]).astype(jnp.int32)
+    current, edge, taps, shifts, near_data, far_data, halo, place, window = plan(
+        estimate, views_data, taps, view_offsets, place, inner, outer
     )
     cover = coverage[0].astype(F32)
     if pair:
         cover = jnp.where(view == 0, cover, cover[::-1])
     weight = cover / jnp.sum(cover)
-    place = jnp.stack([lax.rem(brick, 2), view, low]).astype(jnp.int32)
     ly, lyt, bx, bxt = make_bands(taps, shifts, place, rows, window, width)
     for step in range(ITERS):
         last = step == ITERS - 1
         side, inner_z, inner_side, outer_z, outer_side = halo(current, edge)
-        blur_own, back = near(
-            taps, place, current, side, inner_z, inner_side, near_data, ly, bx
+        blur_far, back = near(
+            taps, place, current, side, inner_z, inner_side, ly, bx, *near_data
         )
         results = far(
-            last, taps, place, weight, outer_z, outer_side, far_data, blur_own, back, current, ly, bx, lyt, bxt
+            last, taps, place, weight, outer_z, outer_side, blur_far, back, current, ly, bx, lyt, bxt, *far_data
         )
         current = results[0]
         edge = None if last else results[1]

time: 127 us -> 128 us (level)
  local copies, waits for them, and re-layouts: 8.7 us -> 1.41 us
  starting transfers between devices: 38.3 us -> 45.5 us
  waiting for transfers between devices: 32.1 us -> 36 us
  other arithmetic: 6.42 us -> 3.8 us
    ppermute x13 -> x14, waiting for transfers between devices: 10.6 us -> 30.5 us  [the longest x4 18.4 us: halo(): inner_side = lax.ppermute(edge, axes, diagonal(inner))]
    ppermute x4, waiting for transfers between devices: 9.11 us -> 0.04 us  [halo(): outer_z = lax.ppermute(current, 'brick', outer)]
    ppermute x4, waiting for transfers between devices: 12.1 us -> 5.39 us  [halo(): side = lax.ppermute(edge, 'view', swap)]
    ppermute x4, starting transfers between devices: 8.85 us -> 15.5 us  [halo(): outer_z = lax.ppermute(current, 'brick', outer)]
    rev x4 -> x0, local copies, waits for them, and re-layouts: 3.73 us -> none  [the longest x1 1.72 us: two_view_plan(): other_near[::-1]]
    another operation x7 -> x0, other arithmetic: 3.26 us -> none  [the longest x3 2.17 us: two_view_plan(): jnp.stack([jnp.concatenate([mine[-R:], mine_near[::-1]]), jnp.concatenate...]
    slice x3 -> x0, local copies, waits for them, and re-layouts: 2.64 us -> none  [the longest x1 1.84 us: two_view_plan(): other[-R:]]
    ppermute x13 -> x14, starting transfers between devices: 24.5 us -> 26.3 us  [the longest x4 11.2 us: halo(): outer_side = lax.ppermute(edge, axes, diagonal(outer))]
  transfers between devices with their start and end apart: 26 -> 27, of which waited for: 12 -> 6; matrix products, arithmetic and copies ran while one was open for 9% -> 1% of each run, Pallas kernels for 16% -> 19%
where the time goes in v1:
time: 128 us
  starting transfers between devices  45.5 us (36%)
  Pallas kernels  40.8 us (32%)
  waiting for transfers between devices  36 us (28%)
  other arithmetic  3.8 us (3%)
  local copies, waits for them, and re-layouts  1.41 us (1%)
    pallas_call x4, Pallas kernels, near(): pl.pallas_call(functools.partial(near_kernel, views), out_shape=[jax.Shap...  21.1 us
    ppermute x4, waiting for transfers between devices, halo(): inner_side = lax.ppermute(edge, axes, diagonal(inner))  18.4 us
    pallas_call x4, Pallas kernels, far(): pl.pallas_call(functools.partial(far_kernel, last, views), out_shape=outs...  17.1 us
    ppermute x4, starting transfers between devices, halo(): outer_z = lax.ppermute(current, 'brick', outer)  15.5 us
    ppermute x4, starting transfers between devices, halo(): outer_side = lax.ppermute(edge, axes, diagonal(outer))  11.2 us
    ppermute x4, waiting for transfers between devices, halo(): outer_side = lax.ppermute(edge, axes, diagonal(outer))  6.72 us
    ppermute x4, starting transfers between devices, halo(): inner_side = lax.ppermute(edge, axes, diagonal(inner))  6.44 us
    ppermute x1, waiting for transfers between devices, two_view_plan(): mine_far = lax.ppermute(mine_out, 'brick', outer)  5.44 us
  transfers between devices with their start and end apart: 27, of which 6 were waited for; matrix products, arithmetic and copies ran while one was open for 1% of the time, Pallas kernels for 19%

profile of v1, /device:TPU:17, one launch (start us, length us, event | category | flops | bytes accessed | tf_op | source)
XLA Modules:
  0.0 127.8 jit_solution(6504284285461793961)
XLA Ops:
  0.0 0.8 reduce_sum.18
  0.8 0.8 divide_reduce_fusion
  1.6 0.1 squeeze_reshape.3
  1.7 0.7 convert_bitcast_fusion.1
  2.3 0.1 pad_maximum_fusion.1
  2.4 1.2 collective-permute-start
  3.7 1.2 copy-done
  4.9 0.6 shard_map.56
  5.6 0.3 collective-permute-start.6
  5.9 1.2 collective-permute-start.7
  7.1 0.6 shard_map.55
  7.8 1.3 collective-permute-start.3
  9.1 0.1 rev.3
  9.2 0.6 fusion
  9.8 0.6 broadcast_divide_fusion.weight
  10.4 0.9 collective-permute-start.5
  11.4 5.4 %collective-permute-done.3.side = f32[16,16,128]{2,1,0:T(8,128)S(1)} collective-permute-done((f32[16,16,128]{2,1,0:T(8,128)S(1)}, f32[16,16,128]{2,1,0:T(8,128)S(1)}, u32[]{:S(2)}, u32[]{:S(2)}) %collective-permute-start.3) | collective-permute-done | bytes 131104 | tf_op jit(solution)/shard_map/ppermute | solution.py:322
  16.7 6.2 %collective-permute-start.1 = (f32[16,64,128]{2,1,0:T(8,128)S(1)}, f32[16,64,128]{2,1,0:T(8,128)S(1)}, u32[]{:S(2)}, u32[]{:S(2)}) collective-permute-start(f32[16,64,128]{2,1,0:T(8,128)S(1)} %get-tuple-element.29.own.est), channel_id=1, source_target_pairs={{2,4},{4,2},{6,8},{8,6},{10,12},{12,10},{14,16},{16,14},{18,20},{2... | collective-permute-start | bytes 1572872 | tf_op jit(solution)/shard_map/ppermute | solution.py:320
  23.1 3.5 %collective-permute-start.10 = (f32[8,80,128]{2,1,0:T(8,128)S(1)}, f32[8,80,128]{2,1,0:T(8,128)S(1)}, u32[]{:S(2)}, u32[]{:S(2)}) collective-permute-start(f32[8,80,128]{2,1,0:T(8,128)S(1)} %get-tuple-element.40), channel_id=1, source_target_pairs={{2,5},{3,4},{4,3},{5,2},{6,9},{7,8},{8,7},{9,6},{10,13},{11,12},{1... | collective-permute-start | bytes 983048 | tf_op jit(solution)/shard_map/ppermute | solution.py:340
  26.6 1.3 collective-permute-start.11
  27.9 2.3 %collective-permute-start.9 = (f32[8,80,128]{2,1,0:T(8,128)S(1)}, f32[8,80,128]{2,1,0:T(8,128)S(1)}, u32[]{:S(2)}, u32[]{:S(2)}) collective-permute-start(f32[8,80,128]{2,1,0:T(8,128)S(1)} %get-tuple-element.39.refs_2_), channel_id=1, source_target_pairs={{2,4},{4,2},{6,8},{8,6},{10,12},{12,10},{14,16},{16,14},{18,20},{2... | collective-permute-start | bytes 983048 | tf_op jit(solution)/shard_map/ppermute | solution.py:339
  30.3 3.2 %collective-permute-start.2 = (f32[16,16,128]{2,1,0:T(8,128)S(1)}, f32[16,16,128]{2,1,0:T(8,128)S(1)}, u32[]{:S(2)}, u32[]{:S(2)}) collective-permute-start(f32[16,16,128]{2,1,0:T(8,128)S(1)} %get-tuple-element.30), channel_id=1, source_target_pairs={{2,5},{3,4},{4,3},{5,2},{6,9},{7,8},{8,7},{9,6},{10,13},{11,12},{1... | collective-permute-start | bytes 393224 | tf_op jit(solution)/shard_map/ppermute | solution.py:321
  33.5 1.4 %bands.1 = (bf16[160,240]{1,0:T(8,128)(2,1)S(1)}, bf16[2,64,240]{2,1,0:T(8,128)(2,1)S(1)}, bf16[2,256,256]{2,1,0:T(8,128)(2,1)S(1)}, bf16[2,256,256]{2,1,0:T(8,128)(2,1)S(1)}) custom-call(f32[2,51]{1,0:T(2,128)S(1)} %bitcast.17, s32[2,2]{1,0:T(2,128)S(1)} %round-nearest-even_convert_fusion.shifts, s32[3]{0:T(128)S(1)} %pad_add_fusion.place.parity), custom_call_target="tpu_custom_call" | custom-call | flops 200000000 | bytes 2000000 | tf_op jit(solution)/shard_map/bands/pallas_call | solution.py:290
  34.9 5.3 %near.4 = (f32[2,16,80,128]{3,2,1,0:T(8,128)S(1)}, f32[2,16,80,128]{3,2,1,0:T(8,128)S(1)}) custom-call(f32[2,51]{1,0:T(2,128)S(1)} %bitcast.18, s32[3]{0:T(128)S(1)} %pad_add_fusion.place.parity, f32[16,64,128]{2,1,0:T(8,128)S(1)} %get-tuple-element.29.own.est, f32[16,16,128]{2,1,0:T(8,128)S(1)} %collective-permute-done.3.side, ...), custom_call_target="tpu_custom_call" | custom-call | flops 1310720000 | bytes 5242880 | tf_op jit(solution)/shard_map/near/pallas_call | solution.py:173
  40.2 6.7 %collective-permute-done.2.side_out = f32[16,16,128]{2,1,0:T(8,128)S(1)} collective-permute-done((f32[16,16,128]{2,1,0:T(8,128)S(1)}, f32[16,16,128]{2,1,0:T(8,128)S(1)}, u32[]{:S(2)}, u32[]{:S(2)}) %collective-permute-start.2) | collective-permute-done | bytes 131104 | tf_op jit(solution)/shard_map/ppermute | solution.py:321
  46.9 5.4 %collective-permute-done.9.refs_0_ = f32[8,80,128]{2,1,0:T(8,128)S(1)} collective-permute-done((f32[8,80,128]{2,1,0:T(8,128)S(1)}, f32[8,80,128]{2,1,0:T(8,128)S(1)}, u32[]{:S(2)}, u32[]{:S(2)}) %collective-permute-start.9) | collective-permute-done | bytes 327712 | tf_op jit(solution)/shard_map/ppermute | solution.py:339
  52.3 4.1 %far.4 = (f32[16,64,128]{2,1,0:T(8,128)S(1)}, f32[16,16,128]{2,1,0:T(8,128)S(1)}) custom-call(f32[2,51]{1,0:T(2,128)S(1)} %bitcast.19, s32[3]{0:T(128)S(1)} %pad_add_fusion.place.parity, f32[2]{0:T(128)S(1)} %broadcast_divide_fusion.weight, f32[16,64,128]{2,1,0:T(8,128)S(1)} %collective-permute-done.1.own_out, ...), custom_call_target="tpu_custom_call" | custom-call | flops 1310720000 | bytes 5242880 | tf_op jit(solution)/shard_map/far/pallas_call | solution.py:194
  56.5 3.6 %collective-permute-start.12 = (f32[16,64,128]{2,1,0:T(8,128)S(1)}, f32[16,64,128]{2,1,0:T(8,128)S(1)}, u32[]{:S(2)}, u32[]{:S(2)}) collective-permute-start(f32[16,64,128]{2,1,0:T(8,128)S(1)} %get-tuple-element.41.own.est), channel_id=1, source_target_pairs={{2,4},{4,2},{6,8},{8,6},{10,12},{12,10},{14,16},{16,14},{18,20},{2... | collective-permute-start | bytes 1572872 | tf_op jit(solution)/shard_map/ppermute | solution.py:320
  60.1 0.3 collective-permute-start.14
  60.5 1.7 %collective-permute-start.16 = (f32[16,16,128]{2,1,0:T(8,128)S(1)}, f32[16,16,128]{2,1,0:T(8,128)S(1)}, u32[]{:S(2)}, u32[]{:S(2)}) collective-permute-start(f32[16,16,128]{2,1,0:T(8,128)S(1)} %get-tuple-element.42), channel_id=1, source_target_pairs={{0,3},{1,2},{2,1},{3,0},{4,7},{5,6},{6,5},{7,4},{8,11},{9,10},{10,... | collective-permute-start | bytes 393224 | tf_op jit(solution)/shard_map/ppermute | solution.py:324
  62.2 2.7 %collective-permute-start.13 = (f32[16,16,128]{2,1,0:T(8,128)S(1)}, f32[16,16,128]{2,1,0:T(8,128)S(1)}, u32[]{:S(2)}, u32[]{:S(2)}) collective-permute-start(f32[16,16,128]{2,1,0:T(8,128)S(1)} %get-tuple-element.42), channel_id=1, source_target_pairs={{2,5},{3,4},{4,3},{5,2},{6,9},{7,8},{8,7},{9,6},{10,13},{11,12},{1... | collective-permute-start | bytes 393224 | tf_op jit(solution)/shard_map/ppermute | solution.py:321
  64.9 6.0 %collective-permute-done.16.side_in = f32[16,16,128]{2,1,0:T(8,128)S(1)} collective-permute-done((f32[16,16,128]{2,1,0:T(8,128)S(1)}, f32[16,16,128]{2,1,0:T(8,128)S(1)}, u32[]{:S(2)}, u32[]{:S(2)}) %collective-permute-start.16) | collective-permute-done | bytes 131104 | tf_op jit(solution)/shard_map/ppermute | solution.py:324
  70.9 5.3 %near.5 = (f32[2,16,80,128]{3,2,1,0:T(8,128)S(1)}, f32[2,16,80,128]{3,2,1,0:T(8,128)S(1)}) custom-call(f32[2,51]{1,0:T(2,128)S(1)} %bitcast.20, s32[3]{0:T(128)S(1)} %pad_add_fusion.place.parity, f32[16,64,128]{2,1,0:T(8,128)S(1)} %get-tuple-element.41.own.est, f32[16,16,128]{2,1,0:T(8,128)S(1)} %collective-permute-done.14.side, ...), custom_call_target="tpu_custom_call" | custom-call | flops 1310720000 | bytes 5242880 | tf_op jit(solution)/shard_map/near/pallas_call | solution.py:173
  76.2 4.1 %far.5 = (f32[16,64,128]{2,1,0:T(8,128)S(1)}, f32[16,16,128]{2,1,0:T(8,128)S(1)}) custom-call(f32[2,51]{1,0:T(2,128)S(1)} %bitcast.21, s32[3]{0:T(128)S(1)} %pad_add_fusion.place.parity, f32[2]{0:T(128)S(1)} %broadcast_divide_fusion.weight, f32[16,64,128]{2,1,0:T(8,128)S(1)} %collective-permute-done.12.own_out, ...), custom_call_target="tpu_custom_call" | custom-call | flops 1310720000 | bytes 5242880 | tf_op jit(solution)/shard_map/far/pallas_call | solution.py:194
  80.4 2.8 %collective-permute-start.17 = (f32[16,64,128]{2,1,0:T(8,128)S(1)}, f32[16,64,128]{2,1,0:T(8,128)S(1)}, u32[]{:S(2)}, u32[]{:S(2)}) collective-permute-start(f32[16,64,128]{2,1,0:T(8,128)S(1)} %get-tuple-element.45.own.est), channel_id=1, source_target_pairs={{2,4},{4,2},{6,8},{8,6},{10,12},{12,10},{14,16},{16,14},{18,20},{2... | collective-permute-start | bytes 1572872 | tf_op jit(solution)/shard_map/ppermute | solution.py:320
  83.2 0.3 collective-permute-start.19
  83.5 1.7 %collective-permute-start.21 = (f32[16,16,128]{2,1,0:T(8,128)S(1)}, f32[16,16,128]{2,1,0:T(8,128)S(1)}, u32[]{:S(2)}, u32[]{:S(2)}) collective-permute-start(f32[16,16,128]{2,1,0:T(8,128)S(1)} %get-tuple-element.46), channel_id=1, source_target_pairs={{0,3},{1,2},{2,1},{3,0},{4,7},{5,6},{6,5},{7,4},{8,11},{9,10},{10,... | collective-permute-start | bytes 393224 | tf_op jit(solution)/shard_map/ppermute | solution.py:324
  85.3 2.9 %collective-permute-start.18 = (f32[16,16,128]{2,1,0:T(8,128)S(1)}, f32[16,16,128]{2,1,0:T(8,128)S(1)}, u32[]{:S(2)}, u32[]{:S(2)}) collective-permute-start(f32[16,16,128]{2,1,0:T(8,128)S(1)} %get-tuple-element.46), channel_id=1, source_target_pairs={{2,5},{3,4},{4,3},{5,2},{6,9},{7,8},{8,7},{9,6},{10,13},{11,12},{1... | collective-permute-start | bytes 393224 | tf_op jit(solution)/shard_map/ppermute | solution.py:321
  88.2 5.8 %collective-permute-done.21.side_in = f32[16,16,128]{2,1,0:T(8,128)S(1)} collective-permute-done((f32[16,16,128]{2,1,0:T(8,128)S(1)}, f32[16,16,128]{2,1,0:T(8,128)S(1)}, u32[]{:S(2)}, u32[]{:S(2)}) %collective-permute-start.21) | collective-permute-done | bytes 131104 | tf_op jit(solution)/shard_map/ppermute | solution.py:324
  94.0 5.3 %near.6 = (f32[2,16,80,128]{3,2,1,0:T(8,128)S(1)}, f32[2,16,80,128]{3,2,1,0:T(8,128)S(1)}) custom-call(f32[2,51]{1,0:T(2,128)S(1)} %bitcast.22, s32[3]{0:T(128)S(1)} %pad_add_fusion.place.parity, f32[16,64,128]{2,1,0:T(8,128)S(1)} %get-tuple-element.45.own.est, f32[16,16,128]{2,1,0:T(8,128)S(1)} %collective-permute-done.19.side, ...), custom_call_target="tpu_custom_call" | custom-call | flops 1310720000 | bytes 5242880 | tf_op jit(solution)/shard_map/near/pallas_call | solution.py:173
  99.3 4.1 %far.6 = (f32[16,64,128]{2,1,0:T(8,128)S(1)}, f32[16,16,128]{2,1,0:T(8,128)S(1)}) custom-call(f32[2,51]{1,0:T(2,128)S(1)} %bitcast.23, s32[3]{0:T(128)S(1)} %pad_add_fusion.place.parity, f32[2]{0:T(128)S(1)} %broadcast_divide_fusion.weight, f32[16,64,128]{2,1,0:T(8,128)S(1)} %collective-permute-done.17.own_out, ...), custom_call_target="tpu_custom_call" | custom-call | flops 1310720000 | bytes 5242880 | tf_op jit(solution)/shard_map/far/pallas_call | solution.py:194
  103.5 2.8 %collective-permute-start.22 = (f32[16,64,128]{2,1,0:T(8,128)S(1)}, f32[16,64,128]{2,1,0:T(8,128)S(1)}, u32[]{:S(2)}, u32[]{:S(2)}) collective-permute-start(f32[16,64,128]{2,1,0:T(8,128)S(1)} %get-tuple-element.49.own.est), channel_id=1, source_target_pairs={{2,4},{4,2},{6,8},{8,6},{10,12},{12,10},{14,16},{16,14},{18,20},{2... | collective-permute-start | bytes 1572872 | tf_op jit(solution)/shard_map/ppermute | solution.py:320
  106.3 0.3 collective-permute-start.24
  106.6 2.1 %collective-permute-start.26 = (f32[16,16,128]{2,1,0:T(8,128)S(1)}, f32[16,16,128]{2,1,0:T(8,128)S(1)}, u32[]{:S(2)}, u32[]{:S(2)}) collective-permute-start(f32[16,16,128]{2,1,0:T(8,128)S(1)} %get-tuple-element.50), channel_id=1, source_target_pairs={{0,3},{1,2},{2,1},{3,0},{4,7},{5,6},{6,5},{7,4},{8,11},{9,10},{10,... | collective-permute-start | bytes 393224 | tf_op jit(solution)/shard_map/ppermute | solution.py:324
  108.7 2.4 %collective-permute-start.23 = (f32[16,16,128]{2,1,0:T(8,128)S(1)}, f32[16,16,128]{2,1,0:T(8,128)S(1)}, u32[]{:S(2)}, u32[]{:S(2)}) collective-permute-start(f32[16,16,128]{2,1,0:T(8,128)S(1)} %get-tuple-element.50), channel_id=1, source_target_pairs={{2,5},{3,4},{4,3},{5,2},{6,9},{7,8},{8,7},{9,6},{10,13},{11,12},{1... | collective-permute-start | bytes 393224 | tf_op jit(solution)/shard_map/ppermute | solution.py:321
  111.1 6.5 %collective-permute-done.26.side_in = f32[16,16,128]{2,1,0:T(8,128)S(1)} collective-permute-done((f32[16,16,128]{2,1,0:T(8,128)S(1)}, f32[16,16,128]{2,1,0:T(8,128)S(1)}, u32[]{:S(2)}, u32[]{:S(2)}) %collective-permute-start.26) | collective-permute-done | bytes 131104 | tf_op jit(solution)/shard_map/ppermute | solution.py:324
  117.6 5.3 %near.7 = (f32[2,16,80,128]{3,2,1,0:T(8,128)S(1)}, f32[2,16,80,128]{3,2,1,0:T(8,128)S(1)}) custom-call(f32[2,51]{1,0:T(2,128)S(1)} %bitcast.24, s32[3]{0:T(128)S(1)} %pad_add_fusion.place.parity, f32[16,64,128]{2,1,0:T(8,128)S(1)} %get-tuple-element.49.own.est, f32[16,16,128]{2,1,0:T(8,128)S(1)} %collective-permute-done.24.side, ...), custom_call_target="tpu_custom_call" | custom-call | flops 1310720000 | bytes 5242880 | tf_op jit(solution)/shard_map/near/pallas_call | solution.py:173
  122.9 4.9 %far.7 = f32[16,64,128]{2,1,0:T(8,128)} custom-call(f32[2,51]{1,0:T(2,128)S(1)} %bitcast.25, s32[3]{0:T(128)S(1)} %pad_add_fusion.place.parity, f32[2]{0:T(128)S(1)} %broadcast_divide_fusion.weight, f32[16,64,128]{2,1,0:T(8,128)S(1)} %collective-permute-done.22.own_out, f32[16,16,128]{2,1,0:T(8,128)S(1)} %collective-permute-done.23.side_out, ...), custom_call_target="tpu_custom_call" | custom-call | flops 1310720000 | bytes 5242880 | tf_op jit(solution)/shard_map/far/pallas_call | solution.py:194
  (36 shorter events, 0.6 us)
Async XLA Ops:
  0.0 9.1 %copy-start.2 = (s32[1,2]{1,0:T(1,128)S(1)}, s32[1,2]{1,0:T(1,128)}, u32[]{:S(2)}) copy-start(s32[1,2]{1,0:T(1,128)} %param.9) | copy-start | bytes 28
  2.4 8.0 %collective-permute-start = (f32[53]{0:T(128)S(1)}, f32[53]{0:T(128)S(1)}, u32[]{:S(2)}, u32[]{:S(2)}) collective-permute-start(f32[53]{0:T(128)S(1)} %pad_maximum_fusion.1), channel_id=1, source_target_pairs={{0,1},{1,0},{2,3},{3,2},{4,5},{5,4},{6,7},{7,6},{8,9},{9,8},{10,11... | collective-permute-start | bytes 644 | tf_op jit(solution)/shard_map/ppermute | solution.py:330
  3.7 1.2 copy-start
  4.9 2.2 %copy-start.1 = (f32[16,64,128]{2,1,0:T(8,128)S(1)}, f32[16,64,128]{2,1,0:T(8,128)}, u32[]{:S(2)}) copy-start(f32[16,64,128]{2,1,0:T(8,128)} %estimate.1) | copy-start | bytes 1572868
  5.6 17.5 %collective-permute-start.6 = (f32[8,80,128]{2,1,0:T(8,128)S(1)}, f32[8,80,128]{2,1,0:T(8,128)S(1)}, u32[]{:S(2)}, u32[]{:S(2)}) collective-permute-start(f32[8,80,128]{2,1,0:T(8,128)S(1)} %get-tuple-element.34), channel_id=1, source_target_pairs={{0,1},{1,0},{2,3},{3,2},{4,5},{5,4},{6,7},{7,6},{8,9},{9,8},{10,11... | collective-permute-start | bytes 983048 | tf_op jit(solution)/shard_map/ppermute | solution.py:337
  5.9 20.7 %collective-permute-start.7 = (f32[8,80,128]{2,1,0:T(8,128)S(1)}, f32[8,80,128]{2,1,0:T(8,128)S(1)}, u32[]{:S(2)}, u32[]{:S(2)}) collective-permute-start(f32[8,80,128]{2,1,0:T(8,128)S(1)} %get-tuple-element.33.refs_0_), channel_id=1, source_target_pairs={{0,2},{2,0},{4,6},{6,4},{8,10},{10,8},{12,14},{14,12},{16,18},{18,... | collective-permute-start | bytes 983048 | tf_op jit(solution)/shard_map/ppermute | solution.py:341
  7.7 20.2 %collective-permute-start.4 = (f32[16,64,128]{2,1,0:T(8,128)S(1)}, f32[16,64,128]{2,1,0:T(8,128)S(1)}, u32[]{:S(2)}, u32[]{:S(2)}) collective-permute-start(f32[16,64,128]{2,1,0:T(8,128)S(1)} %get-tuple-element.29.own.est), channel_id=1, source_target_pairs={{0,2},{2,0},{4,6},{6,4},{8,10},{10,8},{12,14},{14,12},{16,18},{18,... | collective-permute-start | bytes 1572872 | tf_op jit(solution)/shard_map/ppermute | solution.py:323
  7.8 9.0 %collective-permute-start.3 = (f32[16,16,128]{2,1,0:T(8,128)S(1)}, f32[16,16,128]{2,1,0:T(8,128)S(1)}, u32[]{:S(2)}, u32[]{:S(2)}) collective-permute-start(f32[16,16,128]{2,1,0:T(8,128)S(1)} %get-tuple-element.30), channel_id=1, source_target_pairs={{0,1},{1,0},{2,3},{3,2},{4,5},{5,4},{6,7},{7,6},{8,9},{9,8},{10,11... | collective-permute-start | bytes 393224 | tf_op jit(solution)/shard_map/ppermute | solution.py:322
  10.4 12.7 %collective-permute-start.5 = (f32[16,16,128]{2,1,0:T(8,128)S(1)}, f32[16,16,128]{2,1,0:T(8,128)S(1)}, u32[]{:S(2)}, u32[]{:S(2)}) collective-permute-start(f32[16,16,128]{2,1,0:T(8,128)S(1)} %get-tuple-element.30), channel_id=1, source_target_pairs={{0,3},{1,2},{2,1},{3,0},{4,7},{5,6},{6,5},{7,4},{8,11},{9,10},{10,... | collective-permute-start | bytes 393224 | tf_op jit(solution)/shard_map/ppermute | solution.py:324
  16.7 35.6 %collective-permute-start.1 = (f32[16,64,128]{2,1,0:T(8,128)S(1)}, f32[16,64,128]{2,1,0:T(8,128)S(1)}, u32[]{:S(2)}, u32[]{:S(2)}) collective-permute-start(f32[16,64,128]{2,1,0:T(8,128)S(1)} %get-tuple-element.29.own.est), channel_id=1, source_target_pairs={{2,4},{4,2},{6,8},{8,6},{10,12},{12,10},{14,16},{16,14},{18,20},{2... | collective-permute-start | bytes 1572872 | tf_op jit(solution)/shard_map/ppermute | solution.py:320
  23.1 7.2 %collective-permute-start.8 = (f32[8,80,128]{2,1,0:T(8,128)S(1)}, f32[8,80,128]{2,1,0:T(8,128)S(1)}, u32[]{:S(2)}, u32[]{:S(2)}) collective-permute-start(f32[8,80,128]{2,1,0:T(8,128)S(1)} %collective-permute-done.6.refs_1_), channel_id=1, source_target_pairs={{0,2},{2,0},{4,6},{6,4},{8,10},{10,8},{12,14},{14,12},{16,18},{18,... | collective-permute-start | bytes 983048 | tf_op jit(solution)/shard_map/ppermute | solution.py:342
  23.1 29.2 %collective-permute-start.10 = (f32[8,80,128]{2,1,0:T(8,128)S(1)}, f32[8,80,128]{2,1,0:T(8,128)S(1)}, u32[]{:S(2)}, u32[]{:S(2)}) collective-permute-start(f32[8,80,128]{2,1,0:T(8,128)S(1)} %get-tuple-element.40), channel_id=1, source_target_pairs={{2,5},{3,4},{4,3},{5,2},{6,9},{7,8},{8,7},{9,6},{10,13},{11,12},{1... | collective-permute-start | bytes 983048 | tf_op jit(solution)/shard_map/ppermute | solution.py:340
  26.6 25.7 %collective-permute-start.11 = (f32[8,80,128]{2,1,0:T(8,128)S(1)}, f32[8,80,128]{2,1,0:T(8,128)S(1)}, u32[]{:S(2)}, u32[]{:S(2)}) collective-permute-start(f32[8,80,128]{2,1,0:T(8,128)S(1)} %get-tuple-element.40), channel_id=1, source_target_pairs={{0,1},{1,0},{2,3},{3,2},{4,5},{5,4},{6,7},{7,6},{8,9},{9,8},{10,11... | collective-permute-start | bytes 983048 | tf_op jit(solution)/shard_map/ppermute | solution.py:338
  27.9 24.4 %collective-permute-start.9 = (f32[8,80,128]{2,1,0:T(8,128)S(1)}, f32[8,80,128]{2,1,0:T(8,128)S(1)}, u32[]{:S(2)}, u32[]{:S(2)}) collective-permute-start(f32[8,80,128]{2,1,0:T(8,128)S(1)} %get-tuple-element.39.refs_2_), channel_id=1, source_target_pairs={{2,4},{4,2},{6,8},{8,6},{10,12},{12,10},{14,16},{16,14},{18,20},{2... | collective-permute-start | bytes 983048 | tf_op jit(solution)/shard_map/ppermute | solution.py:339
  30.3 16.6 %collective-permute-start.2 = (f32[16,16,128]{2,1,0:T(8,128)S(1)}, f32[16,16,128]{2,1,0:T(8,128)S(1)}, u32[]{:S(2)}, u32[]{:S(2)}) collective-permute-start(f32[16,16,128]{2,1,0:T(8,128)S(1)} %get-tuple-element.30), channel_id=1, source_target_pairs={{2,5},{3,4},{4,3},{5,2},{6,9},{7,8},{8,7},{9,6},{10,13},{11,12},{1... | collective-permute-start | bytes 393224 | tf_op jit(solution)/shard_map/ppermute | solution.py:321
  56.4 14.5 %collective-permute-start.15 = (f32[16,64,128]{2,1,0:T(8,128)S(1)}, f32[16,64,128]{2,1,0:T(8,128)S(1)}, u32[]{:S(2)}, u32[]{:S(2)}) collective-permute-start(f32[16,64,128]{2,1,0:T(8,128)S(1)} %get-tuple-element.41.own.est), channel_id=1, source_target_pairs={{0,2},{2,0},{4,6},{6,4},{8,10},{10,8},{12,14},{14,12},{16,18},{18,... | collective-permute-start | bytes 1572872 | tf_op jit(solution)/shard_map/ppermute | solution.py:323
  56.5 19.7 %collective-permute-start.12 = (f32[16,64,128]{2,1,0:T(8,128)S(1)}, f32[16,64,128]{2,1,0:T(8,128)S(1)}, u32[]{:S(2)}, u32[]{:S(2)}) collective-permute-start(f32[16,64,128]{2,1,0:T(8,128)S(1)} %get-tuple-element.41.own.est), channel_id=1, source_target_pairs={{2,4},{4,2},{6,8},{8,6},{10,12},{12,10},{14,16},{16,14},{18,20},{2... | collective-permute-start | bytes 1572872 | tf_op jit(solution)/shard_map/ppermute | solution.py:320
  60.1 4.8 %collective-permute-start.14 = (f32[16,16,128]{2,1,0:T(8,128)S(1)}, f32[16,16,128]{2,1,0:T(8,128)S(1)}, u32[]{:S(2)}, u32[]{:S(2)}) collective-permute-start(f32[16,16,128]{2,1,0:T(8,128)S(1)} %get-tuple-element.42), channel_id=1, source_target_pairs={{0,1},{1,0},{2,3},{3,2},{4,5},{5,4},{6,7},{7,6},{8,9},{9,8},{10,11... | collective-permute-start | bytes 393224 | tf_op jit(solution)/shard_map/ppermute | solution.py:322
  60.5 10.5 %collective-permute-start.16 = (f32[16,16,128]{2,1,0:T(8,128)S(1)}, f32[16,16,128]{2,1,0:T(8,128)S(1)}, u32[]{:S(2)}, u32[]{:S(2)}) collective-permute-start(f32[16,16,128]{2,1,0:T(8,128)S(1)} %get-tuple-element.42), channel_id=1, source_target_pairs={{0,3},{1,2},{2,1},{3,0},{4,7},{5,6},{6,5},{7,4},{8,11},{9,10},{10,... | collective-permute-start | bytes 393224 | tf_op jit(solution)/shard_map/ppermute | solution.py:324
  62.2 14.0 %collective-permute-start.13 = (f32[16,16,128]{2,1,0:T(8,128)S(1)}, f32[16,16,128]{2,1,0:T(8,128)S(1)}, u32[]{:S(2)}, u32[]{:S(2)}) collective-permute-start(f32[16,16,128]{2,1,0:T(8,128)S(1)} %get-tuple-element.42), channel_id=1, source_target_pairs={{2,5},{3,4},{4,3},{5,2},{6,9},{7,8},{8,7},{9,6},{10,13},{11,12},{1... | collective-permute-start | bytes 393224 | tf_op jit(solution)/shard_map/ppermute | solution.py:321
  80.3 13.7 %collective-permute-start.20 = (f32[16,64,128]{2,1,0:T(8,128)S(1)}, f32[16,64,128]{2,1,0:T(8,128)S(1)}, u32[]{:S(2)}, u32[]{:S(2)}) collective-permute-start(f32[16,64,128]{2,1,0:T(8,128)S(1)} %get-tuple-element.45.own.est), channel_id=1, source_target_pairs={{0,2},{2,0},{4,6},{6,4},{8,10},{10,8},{12,14},{14,12},{16,18},{18,... | collective-permute-start | bytes 1572872 | tf_op jit(solution)/shard_map/ppermute | solution.py:323
  80.4 18.9 %collective-permute-start.17 = (f32[16,64,128]{2,1,0:T(8,128)S(1)}, f32[16,64,128]{2,1,0:T(8,128)S(1)}, u32[]{:S(2)}, u32[]{:S(2)}) collective-permute-start(f32[16,64,128]{2,1,0:T(8,128)S(1)} %get-tuple-element.45.own.est), channel_id=1, source_target_pairs={{2,4},{4,2},{6,8},{8,6},{10,12},{12,10},{14,16},{16,14},{18,20},{2... | collective-permute-start | bytes 1572872 | tf_op jit(solution)/shard_map/ppermute | solution.py:320
  83.2 5.0 %collective-permute-start.19 = (f32[16,16,128]{2,1,0:T(8,128)S(1)}, f32[16,16,128]{2,1,0:T(8,128)S(1)}, u32[]{:S(2)}, u32[]{:S(2)}) collective-permute-start(f32[16,16,128]{2,1,0:T(8,128)S(1)} %get-tuple-element.46), channel_id=1, source_target_pairs={{0,1},{1,0},{2,3},{3,2},{4,5},{5,4},{6,7},{7,6},{8,9},{9,8},{10,11... | collective-permute-start | bytes 393224 | tf_op jit(solution)/shard_map/ppermute | solution.py:322
  83.5 10.5 %collective-permute-start.21 = (f32[16,16,128]{2,1,0:T(8,128)S(1)}, f32[16,16,128]{2,1,0:T(8,128)S(1)}, u32[]{:S(2)}, u32[]{:S(2)}) collective-permute-start(f32[16,16,128]{2,1,0:T(8,128)S(1)} %get-tuple-element.46), channel_id=1, source_target_pairs={{0,3},{1,2},{2,1},{3,0},{4,7},{5,6},{6,5},{7,4},{8,11},{9,10},{10,... | collective-permute-start | bytes 393224 | tf_op jit(solution)/shard_map/ppermute | solution.py:324
  85.3 14.0 %collective-permute-start.18 = (f32[16,16,128]{2,1,0:T(8,128)S(1)}, f32[16,16,128]{2,1,0:T(8,128)S(1)}, u32[]{:S(2)}, u32[]{:S(2)}) collective-permute-start(f32[16,16,128]{2,1,0:T(8,128)S(1)} %get-tuple-element.46), channel_id=1, source_target_pairs={{2,5},{3,4},{4,3},{5,2},{6,9},{7,8},{8,7},{9,6},{10,13},{11,12},{1... | collective-permute-start | bytes 393224 | tf_op jit(solution)/shard_map/ppermute | solution.py:321
  103.4 14.2 %collective-permute-start.25 = (f32[16,64,128]{2,1,0:T(8,128)S(1)}, f32[16,64,128]{2,1,0:T(8,128)S(1)}, u32[]{:S(2)}, u32[]{:S(2)}) collective-permute-start(f32[16,64,128]{2,1,0:T(8,128)S(1)} %get-tuple-element.49.own.est), channel_id=1, source_target_pairs={{0,2},{2,0},{4,6},{6,4},{8,10},{10,8},{12,14},{14,12},{16,18},{18,... | collective-permute-start | bytes 1572872 | tf_op jit(solution)/shard_map/ppermute | solution.py:323
  103.5 19.4 %collective-permute-start.22 = (f32[16,64,128]{2,1,0:T(8,128)S(1)}, f32[16,64,128]{2,1,0:T(8,128)S(1)}, u32[]{:S(2)}, u32[]{:S(2)}) collective-permute-start(f32[16,64,128]{2,1,0:T(8,128)S(1)} %get-tuple-element.49.own.est), channel_id=1, source_target_pairs={{2,4},{4,2},{6,8},{8,6},{10,12},{12,10},{14,16},{16,14},{18,20},{2... | collective-permute-start | bytes 1572872 | tf_op jit(solution)/shard_map/ppermute | solution.py:320
  106.3 4.8 %collective-permute-start.24 = (f32[16,16,128]{2,1,0:T(8,128)S(1)}, f32[16,16,128]{2,1,0:T(8,128)S(1)}, u32[]{:S(2)}, u32[]{:S(2)}) collective-permute-start(f32[16,16,128]{2,1,0:T(8,128)S(1)} %get-tuple-element.50), channel_id=1, source_target_pairs={{0,1},{1,0},{2,3},{3,2},{4,5},{5,4},{6,7},{7,6},{8,9},{9,8},{10,11... | collective-permute-start | bytes 393224 | tf_op jit(solution)/shard_map/ppermute | solution.py:322
  106.6 11.0 %collective-permute-start.26 = (f32[16,16,128]{2,1,0:T(8,128)S(1)}, f32[16,16,128]{2,1,0:T(8,128)S(1)}, u32[]{:S(2)}, u32[]{:S(2)}) collective-permute-start(f32[16,16,128]{2,1,0:T(8,128)S(1)} %get-tuple-element.50), channel_id=1, source_target_pairs={{0,3},{1,2},{2,1},{3,0},{4,7},{5,6},{6,5},{7,4},{8,11},{9,10},{10,... | collective-permute-start | bytes 393224 | tf_op jit(solution)/shard_map/ppermute | solution.py:324
  108.7 14.2 %collective-permute-start.23 = (f32[16,16,128]{2,1,0:T(8,128)S(1)}, f32[16,16,128]{2,1,0:T(8,128)S(1)}, u32[]{:S(2)}, u32[]{:S(2)}) collective-permute-start(f32[16,16,128]{2,1,0:T(8,128)S(1)} %get-tuple-element.50), channel_id=1, source_target_pairs={{2,5},{3,4},{4,3},{5,2},{6,9},{7,8},{8,7},{9,6},{10,13},{11,12},{1... | collective-permute-start | bytes 393224 | tf_op jit(solution)/shard_map/ppermute | solution.py:321
